TPU v7x, 512 devices: a whole 4x8x8 slice. The times are simulated.
512 devices in a mesh: date: 16 (over z, x_hi), trade: 16 (over y, core), path: 2 (over x_lo).
Axes of the slice: x: 4 (x_hi: 2, x_lo: 2; x = x_hi * 2 + x_lo), y: 8, z: 8, core: 2. Of those that a mesh axis runs over, the one named last changes fastest.
Arguments:
- normals: bfloat16 [32, 64, 8192], P('date', None, ('trade', 'path')), may hold values from -6 to 6
- chol: float32 [64, 64], replicated, as said below
- volatility: float32 [64], replicated, may hold values from 0.5 to 2
- start_state: float32 [64], replicated, may hold values from -3 to 3
- basis_map: float32 [64, 128], replicated, may hold values from -0.75 to 0.75
- basis_bias: float32 [128], replicated, may hold values from -3 to 3
- coef: bfloat16 [128, 16384], P(None, 'trade'), may hold values from -0.5 to 0.5
- maturity: int32 [16384], P('trade'), may hold values from 1 to 32
- netting: int32 [16384], P('trade'), may hold values from 0 to 2047, as said below
Outputs:
- exposure: float32 [32, 2048], P('date', 'trade')
Inputs may be any that keep to these rules, and one draw needn't show every extreme that they name: netting sets are whole within a shard of trades: netting[j] // 128 == j // 1024, and every netting set holds at least one trade. `chol`: lower triangular with a positive diagonal.
All inputs are finite; a program needn't handle non-finite values.
Results may differ from a plain program's by a relative error of at most 0.00035.
Values may be sent and summed in bfloat16 or wider, within the bound.
A program may use at most 64 MiB of HBM per device.

v0:
```python
import jax
import jax.numpy as jnp
from jax import lax
from jax.sharding import PartitionSpec as P

NS_DEV = 128


def entering(array, axis, join, neutral):
    place = lax.axis_index(axis)
    gathered = lax.all_gather(array.astype(jnp.bfloat16), axis)
    state = jnp.zeros_like(array) + jnp.asarray(neutral, array.dtype)

    def one(lap, state):
        return join(state, lax.dynamic_index_in_dim(gathered, lap, 0, False).astype(array.dtype))

    return lax.fori_loop(0, place, one, state)


def add_pair(earlier, later):
    return earlier + later


def local_moves(draws, chol, volatility, date_total):
    scale = volatility * jnp.sqrt(jnp.float32(1.0) / date_total)
    moves = jnp.einsum(
        "fg,tgp->tfp", chol, draws.astype(jnp.float32), precision=lax.Precision.HIGHEST
    )
    return jnp.cumsum(moves * scale[None, :, None], axis=0)


def shards(normals, chol, volatility, start_state, basis_map, basis_bias, coef, maturity, netting):
    date_count, factor_count, path_count = normals.shape
    trade_count = coef.shape[1]
    set_count = trade_count * 0 + NS_DEV
    date_total = date_count * lax.axis_size("date")
    path_total = path_count * lax.axis_size("trade") * lax.axis_size("path")
    first_date = lax.axis_index("date") * date_count
    when = first_date + jnp.arange(date_count, dtype=jnp.int32)
    alive = (when[:, None] < maturity[None, :]).astype(jnp.float32)
    local_set = netting - lax.axis_index("trade") * set_count
    member = (local_set[:, None] == jnp.arange(set_count, dtype=jnp.int32)[None, :]).astype(
        jnp.bfloat16
    )
    own_local = local_moves(normals, chol, volatility, date_total)
    empty = jnp.zeros_like(own_local[-1])
    prior = entering(own_local[-1], "date", add_pair, empty)
    states = start_state[None, :, None] + prior[None] + own_local
    pre = jnp.einsum(
        "tfp,fk->tpk",
        lax.all_gather(states, "trade", axis=2, tiled=True),
        basis_map,
        precision=lax.Precision.HIGHEST,
    )
    basis = jnp.tanh(pre + basis_bias[None, None, :]).astype(jnp.bfloat16)
    value = jnp.einsum("tpk,kj->tpj", basis, coef, preferred_element_type=jnp.float32)
    value = (value * alive[:, None, :]).astype(jnp.bfloat16)
    net = jnp.einsum("tpj,js->tps", value, member, preferred_element_type=jnp.float32)
    total = jnp.sum(jnp.maximum(net, 0.0), axis=1)
    summed = lax.psum(total, "path")
    return summed / path_total


def solution(mesh):
    placed = (
        P("date", None, ("trade", "path")),
        P(),
        P(),
        P(),
        P(),
        P(),
        P(None, "trade"),
        P("trade"),
        P("trade"),
    )
    return jax.shard_map(
        shards, mesh=mesh, in_specs=placed, out_specs=P("date", "trade"), check_vma=False
    )
```

profile of v0, /device:TPU:1, one launch (start us, length us, event | category | flops | bytes accessed | tf_op | source)
XLA Modules:
  0.0 125.8 jit_solution(15111759457493451321)
XLA Ops:
  6.5 0.0 copy-start
  6.5 0.0 copy-start.4
  6.5 0.0 copy-start.3
  6.5 0.0 copy-start.5
  6.6 0.0 all-gather.2.cloned.1.call-start
  6.6 0.7 broadcast_multiply_fusion.1
  7.3 1.0 fusion.8
  8.4 0.1 fusion.16
  8.5 43.9 %all_gather.7 = bf16[16,64,256]{2,1,0:T(8,128)(2,1)S(1)} all-gather(bf16[1,64,256]{2,1,0:T(8,128)(2,1)S(1)} %slice.7), channel_id=1, replica_groups=mesh['date'=16,'trade'=16,'path'=2] {'date'}, dimensions={0}, use_global_device_ids=true | all-gather | bytes 557056 | tf_op jit(solution)/shard_map/all_gather | solution.py:11
  52.4 0.0 copy-done.4
  52.4 0.1 broadcast_add_fusion.1
  52.5 0.7 broadcast_add_fusion
  53.2 0.0 all-gather.2.cloned.1.call-update
  53.2 0.0 copy-done.3
  53.2 0.0 copy-done.2
  53.2 0.1 compare_convert_fusion
  53.3 43.9 %all-gather.2.cloned.1.call-done = f32[2,64,4096]{2,1,0:T(8,128)} async-done(((f32[2,64,256]{2,1,0:T(8,128)}), f32[2,64,4096]{2,1,0:T(8,128)}) %all-gather.2.cloned.1.call-update) | async-done | bytes 2097168 | tf_op jit(solution)/shard_map/all_gather | solution.py:51
  97.2 0.0 copy-done.1
  97.2 0.0 copy-done.5
  97.2 8.3 %fusion.6 = bf16[2,4096,128]{2,1,0:T(8,128)(2,1)S(1)} fusion(f32[2,64,4096]{2,1,0:T(8,128)} %all-gather.2.cloned.1.call-done, f32[128]{0:T(128)S(1)} %copy-done.5, f32[64,128]{1,0:T(8,128)S(1)} %copy-done.1), kind=kOutput, calls=%fused_computation.8 | convolution fusion | flops 807403520 | bytes 4227584 | tf_op jit(solution)/shard_map/tfp,fk->tpk/dot_general | solution.py:49
  105.5 0.0 copy-done
  105.5 9.0 %fusion.7 = f32[2,128]{1,0:T(2,128)S(1)} fusion(f32[2,1024]{1,0:T(2,128)S(1)} %compare_convert_fusion, bf16[2,4096,128]{2,1,0:T(8,128)(2,1)S(1)} %fusion.6, bf16[128,1024]{1,0:T(8,128)(2,1)S(1)} %copy-done, s32[1024]{0:T(1024)S(1)} %broadcast_subtract_fusion), kind=kOutput, calls=%fused_computation.9 | convolution fusion | flops 4313972736 | bytes 2372608 | tf_op jit(solution)/shard_map/tpj,js->tps/dot_general | solution.py:58
  114.6 3.8 %psum.7 = f32[2,128]{1,0:T(2,128)S(1)} all-reduce(f32[2,128]{1,0:T(2,128)S(1)} %fusion.7), channel_id=1, replica_groups=mesh['date'=16,'trade'=16,'path'=2] {'path'}, use_global_device_ids=true, to_apply=%region_4.5 | all-reduce | flops 256 | bytes 2048 | tf_op jit(solution)/shard_map/psum | solution.py:60
  118.3 0.6 broadcast_multiply_fusion
  (7 shorter events, 0.0 us)
Async XLA Ops:
  6.5 99.0 %copy-start = (bf16[128,1024]{1,0:T(8,128)(2,1)S(1)}, bf16[128,1024]{1,0:T(8,128)(2,1)}, u32[]{:S(2)}) copy-start(bf16[128,1024]{1,0:T(8,128)(2,1)} %param.17) | copy-start | bytes 786436
  6.5 45.9 %copy-start.4 = (f32[64]{0:T(128)S(1)}, f32[64]{0:T(128)}, u32[]{:S(2)}) copy-start(f32[64]{0:T(128)} %param.14) | copy-start | bytes 772
  6.5 46.7 %copy-start.3 = (s32[1024]{0:T(1024)S(1)}, s32[1024]{0:T(1024)}, u32[]{:S(2)}) copy-start(s32[1024]{0:T(1024)} %param.19) | copy-start | bytes 12292
  6.5 46.7 %copy-start.2 = (s32[1024]{0:T(1024)S(1)}, s32[1024]{0:T(1024)}, u32[]{:S(2)}) copy-start(s32[1024]{0:T(1024)} %param.18) | copy-start | bytes 12292
  6.5 90.6 %copy-start.1 = (f32[64,128]{1,0:T(8,128)S(1)}, f32[64,128]{1,0:T(8,128)}, u32[]{:S(2)}) copy-start(f32[64,128]{1,0:T(8,128)} %param.15) | copy-start | bytes 98308
  6.5 90.6 %copy-start.5 = (f32[128]{0:T(128)S(1)}, f32[128]{0:T(128)}, u32[]{:S(2)}) copy-start(f32[128]{0:T(128)} %param.16) | copy-start | bytes 1540
  6.6 90.6 %all-gather.2.cloned.1.call-start = ((), (), s32[]{:S(2)}) async-start(), calls=%async_computation | async-start | bytes 2228224 | tf_op jit(solution)/shard_map/all_gather | solution.py:51
Sparse Core Ops, SparseCore 0:
  53.3 43.8 all-gather.1
where the time goes:
time: 126 us
  blocking collectives  47.7 us (38%)
  waiting for transfers between devices  43.9 us (35%)
  matrix products  18.4 us (15%)
  between operations  13.5 us (11%)
  other arithmetic  2.22 us (2%)
    all_gather x1, blocking collectives, entering(): gathered = lax.all_gather(array.astype(jnp.bfloat16), axis)  43.9 us
    all_gather x1, waiting for transfers between devices, shards(): lax.all_gather(states, 'trade', axis=2, tiled=True)  43.9 us
    dot_general x1, matrix products, shards(): jnp.einsum('tpj,js->tps', value, member, preferred_element_type=jnp.float32)  9.03 us
    dot_general x1, matrix products, shards(): jnp.einsum('tfp,fk->tpk', lax.all_gather(states, 'trade', axis=2, tiled=T...  8.32 us
    psum x1, blocking collectives, shards(): summed = lax.psum(total, 'path')  3.79 us
  transfers between devices with their start and end apart: 1, of which 1 were waited for; matrix products, arithmetic and copies ran while one was open for 0% of the time, Pallas kernels for 0%

commit v1 on v0

v1 whole, which is shorter than its diff:
```python
import jax
import jax.numpy as jnp
import numpy as np
from jax import lax
from jax.experimental import pallas as pl
from jax.experimental.pallas import tpu as pltpu
from jax.sharding import PartitionSpec as P

MESH = pl.DeviceIdType.MESH
ND = 16
NB = 2
F = 64
K = 128
SETS = 128
SLICE = 16
NJ = 4
HIGH = lax.Precision.HIGHEST


def kernel(
    normals, chol, vol, start, bmap, bias, coef, mat, net,
    out,
    v_norm, v_chol, v_vol, v_start, v_bmap, v_bias, v_coef, v_mat, v_net,
    nt, arrived, sums, zbuf, cbuf, wbuf, part, fin,
    load_sem, send_sem, recv_sem, c_sem,
):
    d, t, p = lax.axis_index("date"), lax.axis_index("trade"), lax.axis_index("path")
    y, c = lax.div(t, 2), lax.rem(t, 2)
    j, par = lax.div(y, 2), lax.rem(y, 2)
    c1, p1 = 1 - c, 1 - p
    twin = t + 2 - 4 * par

    barrier = pltpu.get_barrier_semaphore()

    def hello(where):
        pl.semaphore_signal(barrier, inc=1, device_id=where, device_id_type=MESH)

    def hello_date(i, carry):
        hello({"date": lax.rem(d + i, ND)})
        return carry

    lax.fori_loop(1, ND, hello_date, 0)
    for i in range(1, NJ):
        hello({"trade": lax.rem(t + 4 * i, 16)})
    hello({"trade": twin})
    other = t + 1 - 2 * c
    hello({"trade": other})
    hello({"path": p1})
    hello({"trade": other, "path": p1})

    loads = [
        pltpu.make_async_copy(a, b, load_sem.at[i])
        for i, (a, b) in enumerate(
            (
                (normals, v_norm), (coef, v_coef), (mat, v_mat), (net, v_net), (chol, v_chol),
                (vol, v_vol), (start, v_start), (bmap, v_bmap), (bias, v_bias),
            )
        )
    ]
    for load in loads:
        load.start()

    loads[0].wait()
    flat = v_norm[...].reshape(NB * F, ND * SLICE).astype(jnp.float32)
    nt[...] = flat.T.astype(jnp.bfloat16).reshape(ND, SLICE, NB * F)
    arrived[d] = nt[d]

    for load in loads[1:4]:
        load.wait()
    local_set = v_net[...] - t * SETS
    trades = v_coef.shape[1]
    member = (lax.broadcasted_iota(jnp.int32, (SETS, trades), 0) == local_set)
    member = member.astype(jnp.float32).astype(jnp.bfloat16)
    for b in range(NB):
        alive = (d * NB + b < v_mat[...]).astype(jnp.float32).astype(jnp.bfloat16)
        folded = lax.dot_general(
            v_coef[...] * alive, member, (((1,), (1,)), ((), ())), preferred_element_type=jnp.float32
        )
        high = folded.astype(jnp.bfloat16)
        cbuf[j, c, b, :K, :] = high
        cbuf[j, c, b, K:, :] = (folded - high.astype(jnp.float32)).astype(jnp.bfloat16)

    pl.semaphore_wait(barrier, ND - 1 + NJ - 1 + 4)

    def slice_copy(e):
        return pltpu.make_async_remote_copy(
            src_ref=nt.at[e], dst_ref=arrived.at[d], send_sem=send_sem.at[0], recv_sem=recv_sem.at[0],
            device_id={"date": e}, device_id_type=MESH,
        )

    def send_slice(i, carry):
        slice_copy(lax.rem(d + i, ND)).start()
        return carry

    lax.fori_loop(1, ND, send_slice, 0)

    c_copies = [
        pltpu.make_async_remote_copy(
            src_ref=cbuf.at[j, c], dst_ref=cbuf.at[j, c], send_sem=send_sem.at[1], recv_sem=c_sem.at[i - 1],
            device_id={"trade": lax.rem(t + 4 * i, 16)}, device_id_type=MESH,
        )
        for i in range(1, NJ)
    ]
    for copy in c_copies:
        copy.start()

    def pass_on(slot):
        return pltpu.make_async_remote_copy(
            src_ref=cbuf.at[slot, c], dst_ref=cbuf.at[slot, c], send_sem=send_sem.at[2], recv_sem=recv_sem.at[2],
            device_id={"trade": other}, device_id_type=MESH,
        )

    pass_on(j).start()

    for load in loads[4:]:
        load.wait()
    scale = v_vol[...] * np.float32(np.sqrt(np.float32(1.0) / np.float32(ND * NB)))
    joint = jnp.dot(v_chol[...].T * scale, v_bmap[...], precision=HIGH, preferred_element_type=jnp.float32)
    offset = jnp.dot(v_start[...], v_bmap[...], precision=HIGH, preferred_element_type=jnp.float32) + v_bias[...]
    joint_high = joint.astype(jnp.bfloat16)
    joint_low = (joint - joint_high.astype(jnp.float32)).astype(jnp.bfloat16)
    wbuf[...] = jnp.zeros_like(wbuf)
    for b in range(NB):
        wbuf[pl.ds(b * F, F), pl.ds(b * K, K)] = joint_high
        wbuf[pl.ds(NB * F + b * F, F), pl.ds(b * K, K)] = joint_low
    offsets = jnp.concatenate([offset, offset], axis=1)

    def bytes_of(ref, sem, send):
        whole = pltpu.make_async_remote_copy(
            src_ref=ref, dst_ref=ref, send_sem=sem, recv_sem=sem, device_id={"trade": other}, device_id_type=MESH
        )
        return whole.wait_send() if send else whole.wait_recv()

    bytes_of(arrived.at[pl.ds(0, ND - 1)], recv_sem.at[0], False)
    later_half = lax.broadcasted_iota(jnp.int32, (SLICE, NB * F), 1) >= F
    total = jnp.zeros((SLICE, NB * F), jnp.float32)
    for e in range(ND):
        block = arrived[e].astype(jnp.float32)
        swapped = pltpu.roll(block, F, axis=1)
        pair = block + swapped
        sums[e] = (total + jnp.where(later_half, pair, block)).astype(jnp.bfloat16)
        total = total + pair

    def sums_copy(e, where):
        return pltpu.make_async_remote_copy(
            src_ref=sums.at[e], dst_ref=zbuf.at[par * ND + d], send_sem=send_sem.at[3], recv_sem=recv_sem.at[3],
            device_id={"date": e, "trade": where}, device_id_type=MESH,
        )

    def send_sums(i, carry):
        e = lax.rem(d + i, ND)
        sums_copy(e, t).start()
        sums_copy(e, twin).start()
        return carry

    lax.fori_loop(1, ND, send_sums, 0)
    sums_copy(d, twin).start()
    zbuf[par * ND + d] = sums[d]

    for i in range(1, NJ):
        c_copies[i - 1].wait_recv()
        pass_on(lax.rem(j + NJ - i, NJ)).start()

    bytes_of(zbuf.at[pl.ds(0, 2 * ND - 1)], recv_sem.at[3], False)
    z = zbuf[...].reshape(2 * ND * SLICE, NB * F)
    pre = jnp.dot(jnp.concatenate([z, z], axis=1), wbuf[...], preferred_element_type=jnp.float32)
    basis = jnp.tanh(pre + offsets).astype(jnp.bfloat16)

    bytes_of(cbuf.at[:, c1], recv_sem.at[2], False)
    for b in range(NB):
        own = basis[:, b * K : (b + 1) * K]
        twice = jnp.concatenate([own, own], axis=1)
        for slot in range(NJ):
            both = jnp.concatenate([cbuf[slot, 0, b], cbuf[slot, 1, b]], axis=1)
            values = jnp.dot(twice, both, preferred_element_type=jnp.float32)
            positive = jnp.sum(jnp.maximum(values, 0.0), axis=0, keepdims=True)
            part[slot, 0, b : b + 1, :] = positive[:, :SETS]
            part[slot, 1, b : b + 1, :] = positive[:, SETS:]

    me = j * 4 + c * 2 + p

    def final_copy(to):
        tj, tc, tp = lax.div(to, 4), lax.rem(lax.div(to, 2), 2), lax.rem(to, 2)
        return pltpu.make_async_remote_copy(
            src_ref=part.at[tj, tc], dst_ref=fin.at[me], send_sem=send_sem.at[4], recv_sem=recv_sem.at[4],
            device_id={"trade": tj * 4 + par * 2 + tc, "path": tp}, device_id_type=MESH,
        )

    def send_final(i, carry):
        final_copy(lax.rem(me + i, 16)).start()
        return carry

    lax.fori_loop(1, 16, send_final, 0)
    fin[me] = part[j, c]
    bytes_of(fin.at[pl.ds(0, 15)], recv_sem.at[4], False)
    out[...] = jnp.sum(fin[...], axis=0) * np.float32(1.0 / (ND * SLICE * 32))

    bytes_of(nt.at[pl.ds(0, ND - 1)], send_sem.at[0], True)
    bytes_of(cbuf.at[pl.ds(0, NJ - 1), c], send_sem.at[1], True)
    bytes_of(cbuf.at[:, c], send_sem.at[2], True)
    bytes_of(zbuf.at[pl.ds(0, 2 * ND - 1)], send_sem.at[3], True)
    bytes_of(fin.at[pl.ds(0, 15)], send_sem.at[4], True)


def shards(normals, chol, volatility, start_state, basis_map, basis_bias, coef, maturity, netting):
    args = (
        normals, chol, volatility.reshape(1, -1), start_state.reshape(1, -1), basis_map,
        basis_bias.reshape(1, -1), coef, maturity.reshape(1, -1), netting.reshape(1, -1),
    )
    return pl.pallas_call(
        kernel,
        out_shape=jax.ShapeDtypeStruct((NB, SETS), jnp.float32),
        in_specs=[pl.BlockSpec(memory_space=pl.ANY)] * len(args),
        out_specs=pl.BlockSpec(memory_space=pltpu.VMEM),
        scratch_shapes=[pltpu.VMEM(a.shape, a.dtype) for a in args]
        + [
            pltpu.VMEM((ND, SLICE, NB * F), jnp.bfloat16),
            pltpu.VMEM((ND, SLICE, NB * F), jnp.bfloat16),
            pltpu.VMEM((ND, SLICE, NB * F), jnp.bfloat16),
            pltpu.VMEM((2 * ND, SLICE, NB * F), jnp.bfloat16),
            pltpu.VMEM((NJ, 2, NB, 2 * K, SETS), jnp.bfloat16),
            pltpu.VMEM((2 * NB * F, NB * K), jnp.bfloat16),
            pltpu.VMEM((NJ, 2, NB, SETS), jnp.float32),
            pltpu.VMEM((16, NB, SETS), jnp.float32),
            pltpu.SemaphoreType.DMA((len(args),)),
            pltpu.SemaphoreType.DMA((5,)),
            pltpu.SemaphoreType.DMA((5,)),
            pltpu.SemaphoreType.DMA((NJ - 1,)),
        ],
        compiler_params=pltpu.CompilerParams(
            collective_id=0, has_side_effects=True, vmem_limit_bytes=32 << 20
        ),
    )(*args)


def solution(mesh):
    placed = (
        P("date", None, ("trade", "path")),
        P(),
        P(),
        P(),
        P(),
        P(),
        P(None, "trade"),
        P("trade"),
        P("trade"),
    )
    return jax.shard_map(
        shards, mesh=mesh, in_specs=placed, out_specs=P("date", "trade"), check_vma=False
    )
```

time: 126 us -> 44.8 us (0.36)
  blocking collectives: 47.7 us -> 0 us
  waiting for transfers between devices: 43.9 us -> 0 us
  Pallas kernels: 0 us -> 39.2 us
  matrix products: 18.4 us -> 0 us
  between operations: 13.5 us -> 0.03 us
  local copies, waits for them, and re-layouts: 0.03 us -> 5.22 us
  other arithmetic: 2.22 us -> 0 us
    all_gather x1 -> x0, blocking collectives: 43.9 us -> none  [entering(): gathered = lax.all_gather(array.astype(jnp.bfloat16), axis)]
    all_gather x1 -> x0, waiting for transfers between devices: 43.9 us -> none  [shards(): lax.all_gather(states, 'trade', axis=2, tiled=True)]
    pallas_call x0 -> x1, Pallas kernels: none -> 39.2 us  [shards(): pl.pallas_call(kernel, out_shape=jax.ShapeDtypeStruct((NB, SETS), jnp.flo...]
    dot_general x3 -> x0, matrix products: 18.4 us -> none  [the longest x1 9.03 us: shards(): jnp.einsum('tpj,js->tps', value, member, preferred_element_type=jnp.float32)]
    unnamed x12 -> x19, local copies, waits for them, and re-layouts: 0.02 us -> 5.22 us
    psum x1 -> x0, blocking collectives: 3.79 us -> none  [shards(): summed = lax.psum(total, 'path')]
  transfers between devices with their start and end apart: 1 -> 0, of which waited for: 1 -> 0; matrix products, arithmetic and copies ran while one was open for 0% -> 0% of each run, Pallas kernels for 0% -> 0%
where the time goes in v1:
time: 44.8 us; the launch traced here: 44.5 us
  Pallas kernels  39.2 us (88%)
  local copies, waits for them, and re-layouts  5.22 us (12%)
    pallas_call x1, Pallas kernels, shards(): pl.pallas_call(kernel, out_shape=jax.ShapeDtypeStruct((NB, SETS), jnp.flo...  39.2 us
    unnamed x19, local copies, waits for them, and re-layouts  5.22 us

profile of v1, /device:TPU:1, one launch (start us, length us, event | category | flops | bytes accessed | tf_op | source)
XLA Modules:
  0.0 44.5 jit_solution(1608683996935398394)
XLA Ops:
  0.0 0.0 copy-start.5
  0.0 0.0 copy-start.4
  0.0 0.0 copy-start.6
  0.0 0.0 copy-start.7
  0.0 0.7 %copy-done.5 = s32[1024]{0:T(1024)S(1)} copy-done((s32[1024]{0:T(1024)S(1)}, s32[1024]{0:T(1024)}, u32[]{:S(2)}) %copy-start.5) | copy-done | bytes 4120
  0.7 0.0 copy-done.4
  0.7 0.0 copy-done.6
  0.7 0.0 copy-done.7
  0.7 0.0 copy-start
  0.7 0.9 %copy-done = bf16[128,1024]{1,0:T(8,128)(2,1)S(1)} copy-done((bf16[128,1024]{1,0:T(8,128)(2,1)S(1)}, bf16[128,1024]{1,0:T(8,128)(2,1)}, u32[]{:S(2)}) %copy-start) | copy-done | bytes 262168
  1.7 0.0 copy-start.1
  1.7 0.8 %copy-done.1 = bf16[2,64,256]{2,1,0:T(8,128)(2,1)S(1)} copy-done((bf16[2,64,256]{2,1,0:T(8,128)(2,1)S(1)}, bf16[2,64,256]{2,1,0:T(8,128)(2,1)}, u32[]{:S(2)}) %copy-start.1) | copy-done | bytes 65560
  2.5 0.0 copy-start.2
  2.5 0.8 %copy-done.2 = f32[64,64]{1,0:T(8,128)S(1)} copy-done((f32[64,64]{1,0:T(8,128)S(1)}, f32[64,64]{1,0:T(8,128)}, u32[]{:S(2)}) %copy-start.2) | copy-done | bytes 16408
  3.3 0.0 copy-start.3
  3.3 0.8 %copy-done.3 = f32[64,128]{1,0:T(8,128)S(1)} copy-done((f32[64,128]{1,0:T(8,128)S(1)}, f32[64,128]{1,0:T(8,128)}, u32[]{:S(2)}) %copy-start.3) | copy-done | bytes 32792
  4.0 0.0 copy-start.8
  4.0 0.7 %copy-done.8 = f32[128]{0:T(128)S(1)} copy-done((f32[128]{0:T(128)S(1)}, f32[128]{0:T(128)}, u32[]{:S(2)}) %copy-start.8) | copy-done | bytes 536
  4.7 39.2 %shard_map.91 = f32[2,128]{1,0:T(2,128)S(1)} custom-call(bf16[2,64,256]{2,1,0:T(8,128)(2,1)S(1)} %copy-done.1, f32[64,64]{1,0:T(8,128)S(1)} %copy-done.2, f32[1,64]{1,0:T(1,128)S(1)} %bitcast.7, f32[1,64]{1,0:T(1,128)S(1)} %bitcast.8, f32[64,128]{1,0:T(8,128)S(1)} %copy-done.3, f32[1,128]{1,0:T(1,128)S(1)} %bitcast.9, bf16[128,1024]{1,0:T(8,128)(2,1)S(1)} %copy-done, ...), custom_call_target="tpu_custom_call" | custom-call | tf_op jit(solution)/shard_map/pallas_call | solution.py:210
  43.9 0.6 %copy.11 = f32[2,128]{1,0:T(2,128)} copy(f32[2,128]{1,0:T(2,128)S(1)} %shard_map.91) | data formatting | bytes 2048
Async XLA Ops:
  0.0 0.7 %copy-start.5 = (s32[1024]{0:T(1024)S(1)}, s32[1024]{0:T(1024)}, u32[]{:S(2)}) copy-start(s32[1024]{0:T(1024)} %param.17) | copy-start | bytes 12292
  0.0 0.7 %copy-start.4 = (s32[1024]{0:T(1024)S(1)}, s32[1024]{0:T(1024)}, u32[]{:S(2)}) copy-start(s32[1024]{0:T(1024)} %param.16) | copy-start | bytes 12292
  0.0 0.7 %copy-start.6 = (f32[64]{0:T(128)S(1)}, f32[64]{0:T(128)}, u32[]{:S(2)}) copy-start(f32[64]{0:T(128)} %param.11) | copy-start | bytes 772
  0.0 0.7 %copy-start.7 = (f32[64]{0:T(128)S(1)}, f32[64]{0:T(128)}, u32[]{:S(2)}) copy-start(f32[64]{0:T(128)} %param.12) | copy-start | bytes 772
  0.7 1.0 %copy-start = (bf16[128,1024]{1,0:T(8,128)(2,1)S(1)}, bf16[128,1024]{1,0:T(8,128)(2,1)}, u32[]{:S(2)}) copy-start(bf16[128,1024]{1,0:T(8,128)(2,1)} %coef.1) | copy-start | bytes 786436
  1.7 0.8 %copy-start.1 = (bf16[2,64,256]{2,1,0:T(8,128)(2,1)S(1)}, bf16[2,64,256]{2,1,0:T(8,128)(2,1)}, u32[]{:S(2)}) copy-start(bf16[2,64,256]{2,1,0:T(8,128)(2,1)} %normals.1) | copy-start | bytes 196612
  2.5 0.8 %copy-start.2 = (f32[64,64]{1,0:T(8,128)S(1)}, f32[64,64]{1,0:T(8,128)}, u32[]{:S(2)}) copy-start(f32[64,64]{1,0:T(8,128)} %chol.1) | copy-start | bytes 49156
  3.3 0.8 %copy-start.3 = (f32[64,128]{1,0:T(8,128)S(1)}, f32[64,128]{1,0:T(8,128)}, u32[]{:S(2)}) copy-start(f32[64,128]{1,0:T(8,128)} %bmap.1) | copy-start | bytes 98308
  4.0 0.7 %copy-start.8 = (f32[128]{0:T(128)S(1)}, f32[128]{0:T(128)}, u32[]{:S(2)}) copy-start(f32[128]{0:T(128)} %param.14) | copy-start | bytes 1540

commit v2 on v1

--- a/solution.py
+++ b/solution.py
@@ -210,7 +210,7 @@
     return pl.pallas_call(
         kernel,
         out_shape=jax.ShapeDtypeStruct((NB, SETS), jnp.float32),
-        in_specs=[pl.BlockSpec(memory_space=pl.ANY)] * len(args),
+        in_specs=[pl.BlockSpec(memory_space=pltpu.HBM)] * len(args),
         out_specs=pl.BlockSpec(memory_space=pltpu.VMEM),
         scratch_shapes=[pltpu.VMEM(a.shape, a.dtype) for a in args]
         + [
@@ -228,7 +228,7 @@
             pltpu.SemaphoreType.DMA((NJ - 1,)),
         ],
         compiler_params=pltpu.CompilerParams(
-            collective_id=0, has_side_effects=True, vmem_limit_bytes=32 << 20
+            collective_id=0, has_side_effects=True, vmem_limit_bytes=60 << 20
         ),
     )(*args)
 

time: 44.8 us -> 41.2 us (0.920)
  local copies, waits for them, and re-layouts: 5.22 us -> 1.24 us
  Pallas kernels: 39.2 us -> 39.8 us
    unnamed x19 -> x1, local copies, waits for them, and re-layouts: 5.22 us -> 1.24 us
    pallas_call x1, Pallas kernels: 39.2 us -> 39.8 us  [shards(): pl.pallas_call(kernel, out_shape=jax.ShapeDtypeStruct((NB, SETS), jnp.flo...]
where the time goes in v2:
time: 41.2 us; the launch traced here: 41.1 us
  Pallas kernels  39.8 us (97%)
  local copies, waits for them, and re-layouts  1.24 us (3%)
    pallas_call x1, Pallas kernels, shards(): pl.pallas_call(kernel, out_shape=jax.ShapeDtypeStruct((NB, SETS), jnp.flo...  39.8 us
    unnamed x1, local copies, waits for them, and re-layouts  1.24 us

profile of v2, /device:TPU:1, one launch (start us, length us, event | category | flops | bytes accessed | tf_op | source)
XLA Modules:
  0.0 41.1 jit_solution(2029032056087813034)
XLA Ops:
  0.0 39.8 %shard_map.91 = f32[2,128]{1,0:T(2,128)} custom-call(bf16[2,64,256]{2,1,0:T(8,128)(2,1)} %normals.1, f32[64,64]{1,0:T(8,128)} %chol.1, f32[1,64]{1,0:T(1,128)} %bitcast.7, f32[1,64]{1,0:T(1,128)} %bitcast.8, f32[64,128]{1,0:T(8,128)} %bmap.1, f32[1,128]{1,0:T(1,128)} %bitcast.9, bf16[128,1024]{1,0:T(8,128)(2,1)} %coef.1, s32[1,1024]{1,0:T(1,128)} %bitcast.5, ...), custom_call_target="tpu_custom_call" | custom-call | tf_op jit(solution)/shard_map/pallas_call | solution.py:210
  39.8 1.2 %copy.11 = f32[2,128]{1,0:T(2,128)} copy(f32[2,128]{1,0:T(2,128)} %shard_map.91) | data formatting | bytes 2048

commit v3 on v2

--- a/solution.py
+++ b/solution.py
@@ -12,7 +12,9 @@
 F = 64
 K = 128
 SETS = 128
-SLICE = 16
+NG = 4
+GS = 4
+SLICE = 64
 NJ = 4
 HIGH = lax.Precision.HIGHEST
 
@@ -21,12 +23,13 @@
     normals, chol, vol, start, bmap, bias, coef, mat, net,
     out,
     v_norm, v_chol, v_vol, v_start, v_bmap, v_bias, v_coef, v_mat, v_net,
-    nt, arrived, sums, zbuf, cbuf, wbuf, part, fin,
-    load_sem, send_sem, recv_sem, c_sem,
+    nt, arrived, tmsg, tbuf, sums, zbuf, cbuf, wbuf, part, fin,
+    load_sem, send_sem, recv_sem, c_sem, t_sem, t_sent, ready,
 ):
     d, t, p = lax.axis_index("date"), lax.axis_index("trade"), lax.axis_index("path")
     y, c = lax.div(t, 2), lax.rem(t, 2)
     j, par = lax.div(y, 2), lax.rem(y, 2)
+    g, w = lax.div(d, GS), lax.rem(d, GS)
     c1, p1 = 1 - c, 1 - p
     twin = t + 2 - 4 * par
 
@@ -35,11 +38,14 @@
     def hello(where):
         pl.semaphore_signal(barrier, inc=1, device_id=where, device_id_type=MESH)
 
-    def hello_date(i, carry):
-        hello({"date": lax.rem(d + i, ND)})
-        return carry
-
-    lax.fori_loop(1, ND, hello_date, 0)
+    def mate(i):
+        return g * GS + lax.rem(w + i, GS)
+
+    def later_group(i):
+        return i * GS + w
+
+    for i in range(1, GS):
+        hello({"date": mate(i)})
     for i in range(1, NJ):
         hello({"trade": lax.rem(t + 4 * i, 16)})
     hello({"trade": twin})
@@ -48,6 +54,12 @@
     hello({"path": p1})
     hello({"trade": other, "path": p1})
 
+    def hello_later(i, carry):
+        hello({"date": later_group(i)})
+        return carry
+
+    lax.fori_loop(g + 1, NG, hello_later, 0)
+
     loads = [
         pltpu.make_async_copy(a, b, load_sem.at[i])
         for i, (a, b) in enumerate(
@@ -61,9 +73,9 @@
         load.start()
 
     loads[0].wait()
-    flat = v_norm[...].reshape(NB * F, ND * SLICE).astype(jnp.float32)
-    nt[...] = flat.T.astype(jnp.bfloat16).reshape(ND, SLICE, NB * F)
-    arrived[d] = nt[d]
+    flat = v_norm[...].reshape(NB * F, GS * SLICE).astype(jnp.float32)
+    nt[...] = flat.T.astype(jnp.bfloat16).reshape(GS, SLICE, NB * F)
+    arrived[w] = nt[w]
 
     for load in loads[1:4]:
         load.wait()
@@ -80,19 +92,19 @@
         cbuf[j, c, b, :K, :] = high
         cbuf[j, c, b, K:, :] = (folded - high.astype(jnp.float32)).astype(jnp.bfloat16)
 
-    pl.semaphore_wait(barrier, ND - 1 + NJ - 1 + 4)
-
-    def slice_copy(e):
-        return pltpu.make_async_remote_copy(
-            src_ref=nt.at[e], dst_ref=arrived.at[d], send_sem=send_sem.at[0], recv_sem=recv_sem.at[0],
-            device_id={"date": e}, device_id_type=MESH,
-        )
-
-    def send_slice(i, carry):
-        slice_copy(lax.rem(d + i, ND)).start()
-        return carry
-
-    lax.fori_loop(1, ND, send_slice, 0)
+    pl.semaphore_wait(barrier, GS - 1 + g + NJ - 1 + 4)
+
+    for i in range(1, GS):
+        pltpu.make_async_remote_copy(
+            src_ref=nt.at[lax.rem(w + i, GS)], dst_ref=arrived.at[w], send_sem=send_sem.at[0], recv_sem=recv_sem.at[0],
+            device_id={"date": mate(i)}, device_id_type=MESH,
+        ).start()
+
+    def say_ready(i, carry):
+        pl.semaphore_signal(ready.at[g], inc=1, device_id={"date": later_group(i)}, device_id_type=MESH)
+        return carry
+
+    lax.fori_loop(0, g, say_ready, 0)
 
     c_copies = [
         pltpu.make_async_remote_copy(
@@ -131,38 +143,62 @@
         )
         return whole.wait_send() if send else whole.wait_recv()
 
-    bytes_of(arrived.at[pl.ds(0, ND - 1)], recv_sem.at[0], False)
+    bytes_of(arrived.at[pl.ds(0, GS - 1)], recv_sem.at[0], False)
     later_half = lax.broadcasted_iota(jnp.int32, (SLICE, NB * F), 1) >= F
     total = jnp.zeros((SLICE, NB * F), jnp.float32)
-    for e in range(ND):
+    for e in range(GS):
         block = arrived[e].astype(jnp.float32)
-        swapped = pltpu.roll(block, F, axis=1)
-        pair = block + swapped
+        total = total + (block + pltpu.roll(block, F, axis=1))
+    total_high = total.astype(jnp.bfloat16)
+    tmsg[...] = jnp.where(later_half, total - total_high.astype(jnp.float32), total).astype(jnp.bfloat16)
+
+    def earlier(i, carry):
+        pltpu.make_async_remote_copy(
+            src_ref=tmsg, dst_ref=tbuf.at[i], send_sem=t_sent.at[i], recv_sem=t_sem.at[i],
+            device_id={"trade": other}, device_id_type=MESH,
+        ).wait_recv()
+        both = tbuf[i].astype(jnp.float32)
+        return carry + (both + pltpu.roll(both, F, axis=1))
+
+    total = lax.fori_loop(0, g, earlier, jnp.zeros((SLICE, NB * F), jnp.float32))
+    for e in range(GS):
+        block = arrived[e].astype(jnp.float32)
+        pair = block + pltpu.roll(block, F, axis=1)
         sums[e] = (total + jnp.where(later_half, pair, block)).astype(jnp.bfloat16)
         total = total + pair
 
     def sums_copy(e, where):
         return pltpu.make_async_remote_copy(
-            src_ref=sums.at[e], dst_ref=zbuf.at[par * ND + d], send_sem=send_sem.at[3], recv_sem=recv_sem.at[3],
-            device_id={"date": e, "trade": where}, device_id_type=MESH,
-        )
-
-    def send_sums(i, carry):
-        e = lax.rem(d + i, ND)
+            src_ref=sums.at[e], dst_ref=zbuf.at[par * GS + w], send_sem=send_sem.at[3], recv_sem=recv_sem.at[3],
+            device_id={"date": g * GS + e, "trade": where}, device_id_type=MESH,
+        )
+
+    for i in range(1, GS):
+        e = lax.rem(w + i, GS)
+        sums_copy(e, twin).start()
         sums_copy(e, t).start()
-        sums_copy(e, twin).start()
-        return carry
-
-    lax.fori_loop(1, ND, send_sums, 0)
-    sums_copy(d, twin).start()
-    zbuf[par * ND + d] = sums[d]
+    sums_copy(w, twin).start()
+    zbuf[par * GS + w] = sums[w]
+
+    def total_copy(i):
+        return pltpu.make_async_remote_copy(
+            src_ref=tmsg, dst_ref=tbuf.at[g], send_sem=t_sent.at[i], recv_sem=t_sem.at[g],
+            device_id={"date": later_group(i)}, device_id_type=MESH,
+        )
+
+    def send_total(i, carry):
+        pl.semaphore_wait(ready.at[i], 1)
+        total_copy(i).start()
+        return carry
+
+    lax.fori_loop(g + 1, NG, send_total, 0)
 
     for i in range(1, NJ):
         c_copies[i - 1].wait_recv()
         pass_on(lax.rem(j + NJ - i, NJ)).start()
 
-    bytes_of(zbuf.at[pl.ds(0, 2 * ND - 1)], recv_sem.at[3], False)
-    z = zbuf[...].reshape(2 * ND * SLICE, NB * F)
+    bytes_of(zbuf.at[pl.ds(0, 2 * GS - 1)], recv_sem.at[3], False)
+    z = zbuf[...].reshape(2 * GS * SLICE, NB * F)
     pre = jnp.dot(jnp.concatenate([z, z], axis=1), wbuf[...], preferred_element_type=jnp.float32)
     basis = jnp.tanh(pre + offsets).astype(jnp.bfloat16)
 
@@ -193,13 +229,19 @@
     lax.fori_loop(1, 16, send_final, 0)
     fin[me] = part[j, c]
     bytes_of(fin.at[pl.ds(0, 15)], recv_sem.at[4], False)
-    out[...] = jnp.sum(fin[...], axis=0) * np.float32(1.0 / (ND * SLICE * 32))
-
-    bytes_of(nt.at[pl.ds(0, ND - 1)], send_sem.at[0], True)
+    out[...] = jnp.sum(fin[...], axis=0) * np.float32(1.0 / (GS * SLICE * 32))
+
+    bytes_of(nt.at[pl.ds(0, GS - 1)], send_sem.at[0], True)
     bytes_of(cbuf.at[pl.ds(0, NJ - 1), c], send_sem.at[1], True)
     bytes_of(cbuf.at[:, c], send_sem.at[2], True)
-    bytes_of(zbuf.at[pl.ds(0, 2 * ND - 1)], send_sem.at[3], True)
+    bytes_of(zbuf.at[pl.ds(0, 2 * GS - 1)], send_sem.at[3], True)
     bytes_of(fin.at[pl.ds(0, 15)], send_sem.at[4], True)
+
+    def sent_total(i, carry):
+        total_copy(i).wait_send()
+        return carry
+
+    lax.fori_loop(g + 1, NG, sent_total, 0)
 
 
 def shards(normals, chol, volatility, start_state, basis_map, basis_bias, coef, maturity, netting):
@@ -214,10 +256,12 @@
         out_specs=pl.BlockSpec(memory_space=pltpu.VMEM),
         scratch_shapes=[pltpu.VMEM(a.shape, a.dtype) for a in args]
         + [
-            pltpu.VMEM((ND, SLICE, NB * F), jnp.bfloat16),
-            pltpu.VMEM((ND, SLICE, NB * F), jnp.bfloat16),
-            pltpu.VMEM((ND, SLICE, NB * F), jnp.bfloat16),
-            pltpu.VMEM((2 * ND, SLICE, NB * F), jnp.bfloat16),
+            pltpu.VMEM((GS, SLICE, NB * F), jnp.bfloat16),
+            pltpu.VMEM((GS, SLICE, NB * F), jnp.bfloat16),
+            pltpu.VMEM((SLICE, NB * F), jnp.bfloat16),
+            pltpu.VMEM((NG - 1, SLICE, NB * F), jnp.bfloat16),
+            pltpu.VMEM((GS, SLICE, NB * F), jnp.bfloat16),
+            pltpu.VMEM((2 * GS, SLICE, NB * F), jnp.bfloat16),
             pltpu.VMEM((NJ, 2, NB, 2 * K, SETS), jnp.bfloat16),
             pltpu.VMEM((2 * NB * F, NB * K), jnp.bfloat16),
             pltpu.VMEM((NJ, 2, NB, SETS), jnp.float32),
@@ -226,6 +270,9 @@
             pltpu.SemaphoreType.DMA((5,)),
             pltpu.SemaphoreType.DMA((5,)),
             pltpu.SemaphoreType.DMA((NJ - 1,)),
+            pltpu.SemaphoreType.DMA((NG - 1,)),
+            pltpu.SemaphoreType.DMA((NG,)),
+            pltpu.SemaphoreType.REGULAR((NG,)),
         ],
         compiler_params=pltpu.CompilerParams(
             collective_id=0, has_side_effects=True, vmem_limit_bytes=60 << 20

time: 41.2 us -> 32.7 us (0.79)
  Pallas kernels: 39.8 us -> 31.3 us
    pallas_call x1, Pallas kernels: 39.8 us -> 31.3 us  [shards(): pl.pallas_call(kernel, out_shape=jax.ShapeDtypeStruct((NB, SETS), jnp.flo...]
where the time goes in v3:
time: 32.7 us; the launch traced here: 32.6 us
  Pallas kernels  31.3 us (96%)
  local copies, waits for them, and re-layouts  1.24 us (4%)
    pallas_call x1, Pallas kernels, shards(): pl.pallas_call(kernel, out_shape=jax.ShapeDtypeStruct((NB, SETS), jnp.flo...  31.3 us
    unnamed x1, local copies, waits for them, and re-layouts  1.24 us

profile of v3, /device:TPU:1, one launch (start us, length us, event | category | flops | bytes accessed | tf_op | source)
XLA Modules:
  0.0 32.6 jit_solution(7651330284960016457)
XLA Ops:
  0.0 31.3 %shard_map.91 = f32[2,128]{1,0:T(2,128)} custom-call(bf16[2,64,256]{2,1,0:T(8,128)(2,1)} %normals.1, f32[64,64]{1,0:T(8,128)} %chol.1, f32[1,64]{1,0:T(1,128)} %bitcast.7, f32[1,64]{1,0:T(1,128)} %bitcast.8, f32[64,128]{1,0:T(8,128)} %bmap.1, f32[1,128]{1,0:T(1,128)} %bitcast.9, bf16[128,1024]{1,0:T(8,128)(2,1)} %coef.1, s32[1,1024]{1,0:T(1,128)} %bitcast.5, ...), custom_call_target="tpu_custom_call" | custom-call | tf_op jit(solution)/shard_map/pallas_call | solution.py:252
  31.3 1.2 %copy.11 = f32[2,128]{1,0:T(2,128)} copy(f32[2,128]{1,0:T(2,128)} %shard_map.91) | data formatting | bytes 2048

commit v4 on v3

--- a/solution.py
+++ b/solution.py
@@ -15,6 +15,7 @@
 NG = 4
 GS = 4
 SLICE = 64
+TOP = 127 * 256
 NJ = 4
 HIGH = lax.Precision.HIGHEST
 
@@ -23,7 +24,7 @@
     normals, chol, vol, start, bmap, bias, coef, mat, net,
     out,
     v_norm, v_chol, v_vol, v_start, v_bmap, v_bias, v_coef, v_mat, v_net,
-    nt, arrived, tmsg, tbuf, sums, zbuf, cbuf, wbuf, part, fin,
+    nt, arrived, tmsg, tbuf, sums, zbuf, cbuf, cwide, unit, wbuf, part, fin,
     load_sem, send_sem, recv_sem, c_sem, t_sem, t_sent, ready,
 ):
     d, t, p = lax.axis_index("date"), lax.axis_index("trade"), lax.axis_index("path")
@@ -88,9 +89,9 @@
         folded = lax.dot_general(
             v_coef[...] * alive, member, (((1,), (1,)), ((), ())), preferred_element_type=jnp.float32
         )
-        high = folded.astype(jnp.bfloat16)
-        cbuf[j, c, b, :K, :] = high
-        cbuf[j, c, b, K:, :] = (folded - high.astype(jnp.float32)).astype(jnp.bfloat16)
+        largest = jnp.maximum(jnp.max(jnp.abs(folded), axis=0, keepdims=True), np.float32(1e-30))
+        unit[b : b + 1, :] = largest * np.float32(1.0 / TOP)
+        cbuf[j, c, b] = jnp.round(folded * (np.float32(TOP) / largest)).astype(jnp.int32).astype(jnp.int16)
 
     pl.semaphore_wait(barrier, GS - 1 + g + NJ - 1 + 4)
 
@@ -193,43 +194,52 @@
 
     lax.fori_loop(g + 1, NG, send_total, 0)
 
+    def widen(slot, core):
+        for b in range(NB):
+            whole = cbuf[slot, core, b].astype(jnp.int32).astype(jnp.float32)
+            coarse = jnp.round(whole * np.float32(1 / 256)) * np.float32(256)
+            cwide[slot, core, b, :K, :] = coarse.astype(jnp.bfloat16)
+            cwide[slot, core, b, K:, :] = (whole - coarse).astype(jnp.bfloat16)
+
+    widen(j, c)
     for i in range(1, NJ):
+        slot = lax.rem(j + NJ - i, NJ)
         c_copies[i - 1].wait_recv()
-        pass_on(lax.rem(j + NJ - i, NJ)).start()
+        pass_on(slot).start()
+        widen(slot, c)
+    bytes_of(cbuf.at[:, c1], recv_sem.at[2], False)
+    for slot in range(NJ):
+        widen(slot, c1)
 
     bytes_of(zbuf.at[pl.ds(0, 2 * GS - 1)], recv_sem.at[3], False)
     z = zbuf[...].reshape(2 * GS * SLICE, NB * F)
     pre = jnp.dot(jnp.concatenate([z, z], axis=1), wbuf[...], preferred_element_type=jnp.float32)
     basis = jnp.tanh(pre + offsets).astype(jnp.bfloat16)
-
-    bytes_of(cbuf.at[:, c1], recv_sem.at[2], False)
-    for b in range(NB):
-        own = basis[:, b * K : (b + 1) * K]
-        twice = jnp.concatenate([own, own], axis=1)
-        for slot in range(NJ):
-            both = jnp.concatenate([cbuf[slot, 0, b], cbuf[slot, 1, b]], axis=1)
-            values = jnp.dot(twice, both, preferred_element_type=jnp.float32)
+    twice = [jnp.concatenate([basis[:, b * K : (b + 1) * K]] * 2, axis=1) for b in range(NB)]
+
+    def final_copy(slot, tc, tp):
+        return pltpu.make_async_remote_copy(
+            src_ref=part.at[slot, tc], dst_ref=fin.at[j * 4 + c * 2 + p], send_sem=send_sem.at[4], recv_sem=recv_sem.at[4],
+            device_id={"trade": slot * 4 + par * 2 + tc, "path": tp}, device_id_type=MESH,
+        )
+
+    for i in (2, 1, 3, 0):
+        slot = lax.rem(j + i, NJ)
+        for b in range(NB):
+            both = jnp.concatenate([cwide[slot, 0, b], cwide[slot, 1, b]], axis=1)
+            values = jnp.dot(twice[b], both, preferred_element_type=jnp.float32)
             positive = jnp.sum(jnp.maximum(values, 0.0), axis=0, keepdims=True)
             part[slot, 0, b : b + 1, :] = positive[:, :SETS]
             part[slot, 1, b : b + 1, :] = positive[:, SETS:]
-
-    me = j * 4 + c * 2 + p
-
-    def final_copy(to):
-        tj, tc, tp = lax.div(to, 4), lax.rem(lax.div(to, 2), 2), lax.rem(to, 2)
-        return pltpu.make_async_remote_copy(
-            src_ref=part.at[tj, tc], dst_ref=fin.at[me], send_sem=send_sem.at[4], recv_sem=recv_sem.at[4],
-            device_id={"trade": tj * 4 + par * 2 + tc, "path": tp}, device_id_type=MESH,
-        )
-
-    def send_final(i, carry):
-        final_copy(lax.rem(me + i, 16)).start()
-        return carry
-
-    lax.fori_loop(1, 16, send_final, 0)
-    fin[me] = part[j, c]
+        final_copy(slot, c, p1).start()
+        final_copy(slot, c1, p1).start()
+        final_copy(slot, c1, p).start()
+        if i:
+            final_copy(slot, c, p).start()
+
+    fin[j * 4 + c * 2 + p] = part[j, c]
     bytes_of(fin.at[pl.ds(0, 15)], recv_sem.at[4], False)
-    out[...] = jnp.sum(fin[...], axis=0) * np.float32(1.0 / (GS * SLICE * 32))
+    out[...] = jnp.sum(fin[...], axis=0) * unit[...] * np.float32(1.0 / (GS * SLICE * 32))
 
     bytes_of(nt.at[pl.ds(0, GS - 1)], send_sem.at[0], True)
     bytes_of(cbuf.at[pl.ds(0, NJ - 1), c], send_sem.at[1], True)
@@ -262,7 +272,9 @@
             pltpu.VMEM((NG - 1, SLICE, NB * F), jnp.bfloat16),
             pltpu.VMEM((GS, SLICE, NB * F), jnp.bfloat16),
             pltpu.VMEM((2 * GS, SLICE, NB * F), jnp.bfloat16),
+            pltpu.VMEM((NJ, 2, NB, K, SETS), jnp.int16),
             pltpu.VMEM((NJ, 2, NB, 2 * K, SETS), jnp.bfloat16),
+            pltpu.VMEM((NB, SETS), jnp.float32),
             pltpu.VMEM((2 * NB * F, NB * K), jnp.bfloat16),
             pltpu.VMEM((NJ, 2, NB, SETS), jnp.float32),
             pltpu.VMEM((16, NB, SETS), jnp.float32),

time: 32.7 us -> 29.6 us (0.905)
  the two profiles are of different devices: /device:TPU:1 before, /device:TPU:385 now
where the time goes in v4:
time: 29.6 us; the launch traced here: 29.4 us
  Pallas kernels  28.2 us (95%)
  local copies, waits for them, and re-layouts  1.24 us (4%)
    pallas_call x1, Pallas kernels, shards(): pl.pallas_call(kernel, out_shape=jax.ShapeDtypeStruct((NB, SETS), jnp.flo...  28.2 us
    unnamed x1, local copies, waits for them, and re-layouts  1.24 us

profile of v4, /device:TPU:385, one launch (start us, length us, event | category | flops | bytes accessed | tf_op | source)
XLA Modules:
  0.0 29.4 jit_solution(12991155005328731943)
XLA Ops:
  0.0 28.2 %shard_map.91 = f32[2,128]{1,0:T(2,128)} custom-call(bf16[2,64,256]{2,1,0:T(8,128)(2,1)} %normals.1, f32[64,64]{1,0:T(8,128)} %chol.1, f32[1,64]{1,0:T(1,128)} %bitcast.7, f32[1,64]{1,0:T(1,128)} %bitcast.8, f32[64,128]{1,0:T(8,128)} %bmap.1, f32[1,128]{1,0:T(1,128)} %bitcast.9, bf16[128,1024]{1,0:T(8,128)(2,1)} %coef.1, s32[1,1024]{1,0:T(1,128)} %bitcast.5, ...), custom_call_target="tpu_custom_call" | custom-call | tf_op jit(solution)/shard_map/pallas_call | solution.py:262
  28.2 1.2 %copy.11 = f32[2,128]{1,0:T(2,128)} copy(f32[2,128]{1,0:T(2,128)} %shard_map.91) | data formatting | bytes 2048

commit v5 on v4

--- a/solution.py
+++ b/solution.py
@@ -12,7 +12,6 @@
 F = 64
 K = 128
 SETS = 128
-NG = 4
 GS = 4
 SLICE = 64
 TOP = 127 * 256
@@ -24,7 +23,7 @@
     normals, chol, vol, start, bmap, bias, coef, mat, net,
     out,
     v_norm, v_chol, v_vol, v_start, v_bmap, v_bias, v_coef, v_mat, v_net,
-    nt, arrived, tmsg, tbuf, sums, zbuf, cbuf, cwide, unit, wbuf, part, fin,
+    nt, arrived, ahead, tmsg, tbuf, base, sums, zbuf, cbuf, cwide, unit, wbuf, part, fin,
     load_sem, send_sem, recv_sem, c_sem, t_sem, t_sent, ready,
 ):
     d, t, p = lax.axis_index("date"), lax.axis_index("trade"), lax.axis_index("path")
@@ -42,8 +41,8 @@
     def mate(i):
         return g * GS + lax.rem(w + i, GS)
 
-    def later_group(i):
-        return i * GS + w
+    def counterpart(group):
+        return {"date": group * GS + w}
 
     for i in range(1, GS):
         hello({"date": mate(i)})
@@ -55,11 +54,19 @@
     hello({"path": p1})
     hello({"trade": other, "path": p1})
 
-    def hello_later(i, carry):
-        hello({"date": later_group(i)})
-        return carry
-
-    lax.fori_loop(g + 1, NG, hello_later, 0)
+    @pl.when(g == 0)
+    def _():
+        hello(counterpart(1))
+        hello(counterpart(3))
+
+    @pl.when(g == 1)
+    def _():
+        hello(counterpart(2))
+
+    @pl.when(g == 3)
+    def _():
+        for i in range(GS):
+            hello({"date": 2 * GS + i})
 
     loads = [
         pltpu.make_async_copy(a, b, load_sem.at[i])
@@ -93,7 +100,8 @@
         unit[b : b + 1, :] = largest * np.float32(1.0 / TOP)
         cbuf[j, c, b] = jnp.round(folded * (np.float32(TOP) / largest)).astype(jnp.int32).astype(jnp.int16)
 
-    pl.semaphore_wait(barrier, GS - 1 + g + NJ - 1 + 4)
+    heard = jnp.where(g == 0, 0, 1) + jnp.where(g == 2, GS, 0)
+    pl.semaphore_wait(barrier, GS - 1 + NJ - 1 + 4 + heard)
 
     for i in range(1, GS):
         pltpu.make_async_remote_copy(
@@ -101,11 +109,28 @@
             device_id={"date": mate(i)}, device_id_type=MESH,
         ).start()
 
-    def say_ready(i, carry):
-        pl.semaphore_signal(ready.at[g], inc=1, device_id={"date": later_group(i)}, device_id_type=MESH)
-        return carry
-
-    lax.fori_loop(0, g, say_ready, 0)
+    @pl.when(g == 2)
+    def _():
+        for i in range(GS):
+            pltpu.make_async_remote_copy(
+                src_ref=nt.at[i], dst_ref=ahead.at[w], send_sem=send_sem.at[5], recv_sem=recv_sem.at[5],
+                device_id={"date": 3 * GS + i}, device_id_type=MESH,
+            ).start()
+
+    def say_ready(to, slot):
+        pl.semaphore_signal(ready.at[slot], inc=1, device_id=counterpart(to), device_id_type=MESH)
+
+    @pl.when(g == 1)
+    def _():
+        say_ready(0, 0)
+
+    @pl.when(g == 2)
+    def _():
+        say_ready(1, 0)
+
+    @pl.when(g == 3)
+    def _():
+        say_ready(0, 1)
 
     c_copies = [
         pltpu.make_async_remote_copy(
@@ -146,22 +171,43 @@
 
     bytes_of(arrived.at[pl.ds(0, GS - 1)], recv_sem.at[0], False)
     later_half = lax.broadcasted_iota(jnp.int32, (SLICE, NB * F), 1) >= F
-    total = jnp.zeros((SLICE, NB * F), jnp.float32)
-    for e in range(GS):
-        block = arrived[e].astype(jnp.float32)
-        total = total + (block + pltpu.roll(block, F, axis=1))
-    total_high = total.astype(jnp.bfloat16)
-    tmsg[...] = jnp.where(later_half, total - total_high.astype(jnp.float32), total).astype(jnp.bfloat16)
-
-    def earlier(i, carry):
-        pltpu.make_async_remote_copy(
-            src_ref=tmsg, dst_ref=tbuf.at[i], send_sem=t_sent.at[i], recv_sem=t_sem.at[i],
-            device_id={"trade": other}, device_id_type=MESH,
-        ).wait_recv()
-        both = tbuf[i].astype(jnp.float32)
-        return carry + (both + pltpu.roll(both, F, axis=1))
-
-    total = lax.fori_loop(0, g, earlier, jnp.zeros((SLICE, NB * F), jnp.float32))
+
+    def twofold(message):
+        message = message.astype(jnp.float32)
+        return message + pltpu.roll(message, F, axis=1)
+
+    def terms(value):
+        high = value.astype(jnp.bfloat16).astype(jnp.float32)
+        return jnp.where(later_half, value - high, value).astype(jnp.bfloat16)
+
+    own = sum(twofold(arrived[e]) for e in range(GS))
+    tmsg[0] = terms(own)
+
+    def total_copy(to, message, slot):
+        return pltpu.make_async_remote_copy(
+            src_ref=tmsg.at[message], dst_ref=tbuf.at[slot], send_sem=t_sent.at[message], recv_sem=t_sem.at[slot],
+            device_id=counterpart(to), device_id_type=MESH,
+        )
+
+    @pl.when(g == 0)
+    def _():
+        base[...] = jnp.zeros_like(base)
+
+    @pl.when(g == 1)
+    def _():
+        total_copy(0, 0, 1).start()
+
+    @pl.when(g > 0)
+    def _():
+        total_copy(0, 0, 0).wait_recv()
+        base[...] = twofold(tbuf[0])
+
+    @pl.when(g == 3)
+    def _():
+        bytes_of(ahead, recv_sem.at[5], False)
+        base[...] += sum(twofold(ahead[e]) for e in range(GS))
+
+    total = base[...]
     for e in range(GS):
         block = arrived[e].astype(jnp.float32)
         pair = block + pltpu.roll(block, F, axis=1)
@@ -181,18 +227,20 @@
     sums_copy(w, twin).start()
     zbuf[par * GS + w] = sums[w]
 
-    def total_copy(i):
-        return pltpu.make_async_remote_copy(
-            src_ref=tmsg, dst_ref=tbuf.at[g], send_sem=t_sent.at[i], recv_sem=t_sem.at[g],
-            device_id={"date": later_group(i)}, device_id_type=MESH,
-        )
-
-    def send_total(i, carry):
-        pl.semaphore_wait(ready.at[i], 1)
-        total_copy(i).start()
-        return carry
-
-    lax.fori_loop(g + 1, NG, send_total, 0)
+    @pl.when(g == 0)
+    def _():
+        pl.semaphore_wait(ready.at[0], 1)
+        total_copy(1, 0, 0).start()
+        total_copy(1, 0, 1).wait_recv()
+        tmsg[1] = terms(own + twofold(tbuf[1]))
+        pl.semaphore_wait(ready.at[1], 1)
+        total_copy(3, 1, 0).start()
+
+    @pl.when(g == 1)
+    def _():
+        tmsg[1] = terms(total)
+        pl.semaphore_wait(ready.at[0], 1)
+        total_copy(2, 1, 0).start()
 
     def widen(slot, core):
         for b in range(NB):
@@ -247,11 +295,14 @@
     bytes_of(zbuf.at[pl.ds(0, 2 * GS - 1)], send_sem.at[3], True)
     bytes_of(fin.at[pl.ds(0, 15)], send_sem.at[4], True)
 
-    def sent_total(i, carry):
-        total_copy(i).wait_send()
-        return carry
-
-    lax.fori_loop(g + 1, NG, sent_total, 0)
+    @pl.when(g < 2)
+    def _():
+        total_copy(1, 0, 0).wait_send()
+        total_copy(1, 1, 0).wait_send()
+
+    @pl.when(g == 2)
+    def _():
+        bytes_of(nt, send_sem.at[5], True)
 
 
 def shards(normals, chol, volatility, start_state, basis_map, basis_bias, coef, maturity, netting):
@@ -268,8 +319,10 @@
         + [
             pltpu.VMEM((GS, SLICE, NB * F), jnp.bfloat16),
             pltpu.VMEM((GS, SLICE, NB * F), jnp.bfloat16),
-            pltpu.VMEM((SLICE, NB * F), jnp.bfloat16),
-            pltpu.VMEM((NG - 1, SLICE, NB * F), jnp.bfloat16),
+            pltpu.VMEM((GS, SLICE, NB * F), jnp.bfloat16),
+            pltpu.VMEM((2, SLICE, NB * F), jnp.bfloat16),
+            pltpu.VMEM((2, SLICE, NB * F), jnp.bfloat16),
+            pltpu.VMEM((SLICE, NB * F), jnp.float32),
             pltpu.VMEM((GS, SLICE, NB * F), jnp.bfloat16),
             pltpu.VMEM((2 * GS, SLICE, NB * F), jnp.bfloat16),
             pltpu.VMEM((NJ, 2, NB, K, SETS), jnp.int16),
@@ -279,12 +332,12 @@
             pltpu.VMEM((NJ, 2, NB, SETS), jnp.float32),
             pltpu.VMEM((16, NB, SETS), jnp.float32),
             pltpu.SemaphoreType.DMA((len(args),)),
-            pltpu.SemaphoreType.DMA((5,)),
-            pltpu.SemaphoreType.DMA((5,)),
+            pltpu.SemaphoreType.DMA((6,)),
+            pltpu.SemaphoreType.DMA((6,)),
             pltpu.SemaphoreType.DMA((NJ - 1,)),
-            pltpu.SemaphoreType.DMA((NG - 1,)),
-            pltpu.SemaphoreType.DMA((NG,)),
-            pltpu.SemaphoreType.REGULAR((NG,)),
+            pltpu.SemaphoreType.DMA((2,)),
+            pltpu.SemaphoreType.DMA((2,)),
+            pltpu.SemaphoreType.REGULAR((2,)),
         ],
         compiler_params=pltpu.CompilerParams(
             collective_id=0, has_side_effects=True, vmem_limit_bytes=60 << 20

time: 29.6 us -> 27.5 us (0.929)
  the two profiles are of different devices: /device:TPU:385 before, /device:TPU:1 now
where the time goes in v5:
time: 27.5 us; the launch traced here: 27 us
  Pallas kernels  25.8 us (94%)
  local copies, waits for them, and re-layouts  1.24 us (5%)
    pallas_call x1, Pallas kernels, shards(): pl.pallas_call(kernel, out_shape=jax.ShapeDtypeStruct((NB, SETS), jnp.flo...  25.8 us
    unnamed x1, local copies, waits for them, and re-layouts  1.24 us

profile of v5, /device:TPU:1, one launch (start us, length us, event | category | flops | bytes accessed | tf_op | source)
XLA Modules:
  0.0 27.0 jit_solution(12246697031532550740)
XLA Ops:
  0.0 25.8 %shard_map.91 = f32[2,128]{1,0:T(2,128)} custom-call(bf16[2,64,256]{2,1,0:T(8,128)(2,1)} %normals.1, f32[64,64]{1,0:T(8,128)} %chol.1, f32[1,64]{1,0:T(1,128)} %bitcast.7, f32[1,64]{1,0:T(1,128)} %bitcast.8, f32[64,128]{1,0:T(8,128)} %bmap.1, f32[1,128]{1,0:T(1,128)} %bitcast.9, bf16[128,1024]{1,0:T(8,128)(2,1)} %coef.1, s32[1,1024]{1,0:T(1,128)} %bitcast.5, ...), custom_call_target="tpu_custom_call" | custom-call | tf_op jit(solution)/shard_map/pallas_call | solution.py:313
  25.8 1.2 %copy.11 = f32[2,128]{1,0:T(2,128)} copy(f32[2,128]{1,0:T(2,128)} %shard_map.91) | data formatting | bytes 2048

commit v6 on v5

--- a/solution.py
+++ b/solution.py
@@ -28,10 +28,20 @@
 ):
     d, t, p = lax.axis_index("date"), lax.axis_index("trade"), lax.axis_index("path")
     y, c = lax.div(t, 2), lax.rem(t, 2)
-    j, par = lax.div(y, 2), lax.rem(y, 2)
+    par = lax.rem(y, 2)
+    side = 2 * par - 1
     g, w = lax.div(d, GS), lax.rem(d, GS)
     c1, p1 = 1 - c, 1 - p
-    twin = t + 2 - 4 * par
+    twin = t - 2 * side
+
+    def row(steps):
+        return lax.rem(t + 2 * steps + 16, 16)
+
+    def valued(slot):
+        return row(side * slot)
+
+    def valuer(slot):
+        return row(side * slot * (1 if slot % 2 else -1))
 
     barrier = pltpu.get_barrier_semaphore()
 
@@ -39,19 +49,18 @@
         pl.semaphore_signal(barrier, inc=1, device_id=where, device_id_type=MESH)
 
     def mate(i):
-        return g * GS + lax.rem(w + i, GS)
+        return {"date": g * GS + lax.rem(w + i, GS), "path": p1}
 
     def counterpart(group):
         return {"date": group * GS + w}
 
-    for i in range(1, GS):
-        hello({"date": mate(i)})
-    for i in range(1, NJ):
-        hello({"trade": lax.rem(t + 4 * i, 16)})
+    for i in range(GS):
+        hello(mate(i))
+    for i in (1, 2, 3, -2):
+        hello({"trade": row(side * i)})
     hello({"trade": twin})
     other = t + 1 - 2 * c
     hello({"trade": other})
-    hello({"path": p1})
     hello({"trade": other, "path": p1})
 
     @pl.when(g == 0)
@@ -66,7 +75,7 @@
     @pl.when(g == 3)
     def _():
         for i in range(GS):
-            hello({"date": 2 * GS + i})
+            hello({"date": 2 * GS + i, "path": p1})
 
     loads = [
         pltpu.make_async_copy(a, b, load_sem.at[i])
@@ -83,7 +92,6 @@
     loads[0].wait()
     flat = v_norm[...].reshape(NB * F, GS * SLICE).astype(jnp.float32)
     nt[...] = flat.T.astype(jnp.bfloat16).reshape(GS, SLICE, NB * F)
-    arrived[w] = nt[w]
 
     for load in loads[1:4]:
         load.wait()
@@ -98,15 +106,15 @@
         )
         largest = jnp.maximum(jnp.max(jnp.abs(folded), axis=0, keepdims=True), np.float32(1e-30))
         unit[b : b + 1, :] = largest * np.float32(1.0 / TOP)
-        cbuf[j, c, b] = jnp.round(folded * (np.float32(TOP) / largest)).astype(jnp.int32).astype(jnp.int16)
+        cbuf[0, c, b] = jnp.round(folded * (np.float32(TOP) / largest)).astype(jnp.int32).astype(jnp.int16)
 
     heard = jnp.where(g == 0, 0, 1) + jnp.where(g == 2, GS, 0)
-    pl.semaphore_wait(barrier, GS - 1 + NJ - 1 + 4 + heard)
-
-    for i in range(1, GS):
+    pl.semaphore_wait(barrier, GS + 4 + 3 + heard)
+
+    for i in (2, 3, 1, 0):
         pltpu.make_async_remote_copy(
             src_ref=nt.at[lax.rem(w + i, GS)], dst_ref=arrived.at[w], send_sem=send_sem.at[0], recv_sem=recv_sem.at[0],
-            device_id={"date": mate(i)}, device_id_type=MESH,
+            device_id=mate(i), device_id_type=MESH,
         ).start()
 
     @pl.when(g == 2)
@@ -114,7 +122,7 @@
         for i in range(GS):
             pltpu.make_async_remote_copy(
                 src_ref=nt.at[i], dst_ref=ahead.at[w], send_sem=send_sem.at[5], recv_sem=recv_sem.at[5],
-                device_id={"date": 3 * GS + i}, device_id_type=MESH,
+                device_id={"date": 3 * GS + i, "path": p1}, device_id_type=MESH,
             ).start()
 
     def say_ready(to, slot):
@@ -134,8 +142,8 @@
 
     c_copies = [
         pltpu.make_async_remote_copy(
-            src_ref=cbuf.at[j, c], dst_ref=cbuf.at[j, c], send_sem=send_sem.at[1], recv_sem=c_sem.at[i - 1],
-            device_id={"trade": lax.rem(t + 4 * i, 16)}, device_id_type=MESH,
+            src_ref=cbuf.at[0, c], dst_ref=cbuf.at[i, c], send_sem=send_sem.at[1], recv_sem=c_sem.at[i - 1],
+            device_id={"trade": valuer(i)}, device_id_type=MESH,
         )
         for i in range(1, NJ)
     ]
@@ -148,7 +156,7 @@
             device_id={"trade": other}, device_id_type=MESH,
         )
 
-    pass_on(j).start()
+    pass_on(0).start()
 
     for load in loads[4:]:
         load.wait()
@@ -169,7 +177,7 @@
         )
         return whole.wait_send() if send else whole.wait_recv()
 
-    bytes_of(arrived.at[pl.ds(0, GS - 1)], recv_sem.at[0], False)
+    bytes_of(arrived, recv_sem.at[0], False)
     later_half = lax.broadcasted_iota(jnp.int32, (SLICE, NB * F), 1) >= F
 
     def twofold(message):
@@ -214,18 +222,12 @@
         sums[e] = (total + jnp.where(later_half, pair, block)).astype(jnp.bfloat16)
         total = total + pair
 
-    def sums_copy(e, where):
-        return pltpu.make_async_remote_copy(
-            src_ref=sums.at[e], dst_ref=zbuf.at[par * GS + w], send_sem=send_sem.at[3], recv_sem=recv_sem.at[3],
-            device_id={"date": g * GS + e, "trade": where}, device_id_type=MESH,
-        )
-
-    for i in range(1, GS):
-        e = lax.rem(w + i, GS)
-        sums_copy(e, twin).start()
-        sums_copy(e, t).start()
-    sums_copy(w, twin).start()
-    zbuf[par * GS + w] = sums[w]
+    for i in (2, 3, 1, 0):
+        for where in (twin, t):
+            pltpu.make_async_remote_copy(
+                src_ref=sums.at[lax.rem(w + i, GS)], dst_ref=zbuf.at[par * GS + w], send_sem=send_sem.at[3], recv_sem=recv_sem.at[3],
+                device_id={**mate(i), "trade": where}, device_id_type=MESH,
+            ).start()
 
     @pl.when(g == 0)
     def _():
@@ -249,50 +251,42 @@
             cwide[slot, core, b, :K, :] = coarse.astype(jnp.bfloat16)
             cwide[slot, core, b, K:, :] = (whole - coarse).astype(jnp.bfloat16)
 
-    widen(j, c)
-    for i in range(1, NJ):
-        slot = lax.rem(j + NJ - i, NJ)
-        c_copies[i - 1].wait_recv()
+    widen(0, c)
+    for slot in range(1, NJ):
+        c_copies[slot - 1].wait_recv()
         pass_on(slot).start()
         widen(slot, c)
     bytes_of(cbuf.at[:, c1], recv_sem.at[2], False)
     for slot in range(NJ):
         widen(slot, c1)
 
-    bytes_of(zbuf.at[pl.ds(0, 2 * GS - 1)], recv_sem.at[3], False)
+    bytes_of(zbuf, recv_sem.at[3], False)
     z = zbuf[...].reshape(2 * GS * SLICE, NB * F)
     pre = jnp.dot(jnp.concatenate([z, z], axis=1), wbuf[...], preferred_element_type=jnp.float32)
     basis = jnp.tanh(pre + offsets).astype(jnp.bfloat16)
     twice = [jnp.concatenate([basis[:, b * K : (b + 1) * K]] * 2, axis=1) for b in range(NB)]
 
-    def final_copy(slot, tc, tp):
-        return pltpu.make_async_remote_copy(
-            src_ref=part.at[slot, tc], dst_ref=fin.at[j * 4 + c * 2 + p], send_sem=send_sem.at[4], recv_sem=recv_sem.at[4],
-            device_id={"trade": slot * 4 + par * 2 + tc, "path": tp}, device_id_type=MESH,
-        )
-
-    for i in (2, 1, 3, 0):
-        slot = lax.rem(j + i, NJ)
+    for slot in range(NJ - 1, -1, -1):
         for b in range(NB):
             both = jnp.concatenate([cwide[slot, 0, b], cwide[slot, 1, b]], axis=1)
             values = jnp.dot(twice[b], both, preferred_element_type=jnp.float32)
             positive = jnp.sum(jnp.maximum(values, 0.0), axis=0, keepdims=True)
             part[slot, 0, b : b + 1, :] = positive[:, :SETS]
             part[slot, 1, b : b + 1, :] = positive[:, SETS:]
-        final_copy(slot, c, p1).start()
-        final_copy(slot, c1, p1).start()
-        final_copy(slot, c1, p).start()
-        if i:
-            final_copy(slot, c, p).start()
-
-    fin[j * 4 + c * 2 + p] = part[j, c]
+        for tc, tp in ((c1, p1), (c, p1), (c1, p), (c, p))[: 4 if slot else 3]:
+            pltpu.make_async_remote_copy(
+                src_ref=part.at[slot, tc], dst_ref=fin.at[slot * 4 + c * 2 + p], send_sem=send_sem.at[4], recv_sem=recv_sem.at[4],
+                device_id={"trade": valued(slot) - c + tc, "path": tp}, device_id_type=MESH,
+            ).start()
+
+    fin[c * 2 + p] = part[0, c]
     bytes_of(fin.at[pl.ds(0, 15)], recv_sem.at[4], False)
     out[...] = jnp.sum(fin[...], axis=0) * unit[...] * np.float32(1.0 / (GS * SLICE * 32))
 
-    bytes_of(nt.at[pl.ds(0, GS - 1)], send_sem.at[0], True)
+    bytes_of(nt, send_sem.at[0], True)
     bytes_of(cbuf.at[pl.ds(0, NJ - 1), c], send_sem.at[1], True)
     bytes_of(cbuf.at[:, c], send_sem.at[2], True)
-    bytes_of(zbuf.at[pl.ds(0, 2 * GS - 1)], send_sem.at[3], True)
+    bytes_of(zbuf, send_sem.at[3], True)
     bytes_of(fin.at[pl.ds(0, 15)], send_sem.at[4], True)
 
     @pl.when(g < 2)

time: 27.5 us -> 26.8 us (0.975)
  the two profiles are of different devices: /device:TPU:1 before, /device:TPU:384 now
where the time goes in v6:
time: 26.8 us; the launch traced here: 26.7 us
  Pallas kernels  25.4 us (95%)
  local copies, waits for them, and re-layouts  1.24 us (5%)
    pallas_call x1, Pallas kernels, shards(): pl.pallas_call(kernel, out_shape=jax.ShapeDtypeStruct((NB, SETS), jnp.flo...  25.4 us
    unnamed x1, local copies, waits for them, and re-layouts  1.24 us

profile of v6, /device:TPU:384, one launch (start us, length us, event | category | flops | bytes accessed | tf_op | source)
XLA Modules:
  0.0 26.7 jit_solution(227966141078126426)
XLA Ops:
  0.0 25.4 %shard_map.91 = f32[2,128]{1,0:T(2,128)} custom-call(bf16[2,64,256]{2,1,0:T(8,128)(2,1)} %normals.1, f32[64,64]{1,0:T(8,128)} %chol.1, f32[1,64]{1,0:T(1,128)} %bitcast.7, f32[1,64]{1,0:T(1,128)} %bitcast.8, f32[64,128]{1,0:T(8,128)} %bmap.1, f32[1,128]{1,0:T(1,128)} %bitcast.9, bf16[128,1024]{1,0:T(8,128)(2,1)} %coef.1, s32[1,1024]{1,0:T(1,128)} %bitcast.5, ...), custom_call_target="tpu_custom_call" | custom-call | tf_op jit(solution)/shard_map/pallas_call | solution.py:307
  25.4 1.2 %copy.11 = f32[2,128]{1,0:T(2,128)} copy(f32[2,128]{1,0:T(2,128)} %shard_map.91) | data formatting | bytes 2048

commit v7 on v6

--- a/solution.py
+++ b/solution.py
@@ -72,10 +72,16 @@
     def _():
         hello(counterpart(2))
 
-    @pl.when(g == 3)
+    outer = jnp.logical_or(g == 0, g == 3)
+    beside = jnp.where(g < 2, 1 - g, 5 - g)
+
+    def across(i):
+        return {"date": beside * GS + lax.rem(w + i, GS), "path": p1}
+
+    @pl.when(outer)
     def _():
         for i in range(GS):
-            hello({"date": 2 * GS + i, "path": p1})
+            hello(across(i))
 
     loads = [
         pltpu.make_async_copy(a, b, load_sem.at[i])
@@ -108,7 +114,7 @@
         unit[b : b + 1, :] = largest * np.float32(1.0 / TOP)
         cbuf[0, c, b] = jnp.round(folded * (np.float32(TOP) / largest)).astype(jnp.int32).astype(jnp.int16)
 
-    heard = jnp.where(g == 0, 0, 1) + jnp.where(g == 2, GS, 0)
+    heard = jnp.where(g == 0, 0, 1) + jnp.where(outer, 0, GS)
     pl.semaphore_wait(barrier, GS + 4 + 3 + heard)
 
     for i in (2, 3, 1, 0):
@@ -117,12 +123,12 @@
             device_id=mate(i), device_id_type=MESH,
         ).start()
 
-    @pl.when(g == 2)
+    @pl.when(jnp.logical_not(outer))
     def _():
         for i in range(GS):
             pltpu.make_async_remote_copy(
-                src_ref=nt.at[i], dst_ref=ahead.at[w], send_sem=send_sem.at[5], recv_sem=recv_sem.at[5],
-                device_id={"date": 3 * GS + i, "path": p1}, device_id_type=MESH,
+                src_ref=nt.at[lax.rem(w + i, GS)], dst_ref=ahead.at[w], send_sem=send_sem.at[5], recv_sem=recv_sem.at[5],
+                device_id=across(i), device_id_type=MESH,
             ).start()
 
     def say_ready(to, slot):
@@ -191,9 +197,9 @@
     own = sum(twofold(arrived[e]) for e in range(GS))
     tmsg[0] = terms(own)
 
-    def total_copy(to, message, slot):
+    def total_copy(to, message):
         return pltpu.make_async_remote_copy(
-            src_ref=tmsg.at[message], dst_ref=tbuf.at[slot], send_sem=t_sent.at[message], recv_sem=t_sem.at[slot],
+            src_ref=tmsg.at[message], dst_ref=tbuf, send_sem=t_sent.at[message], recv_sem=t_sem.at[0],
             device_id=counterpart(to), device_id_type=MESH,
         )
 
@@ -201,14 +207,10 @@
     def _():
         base[...] = jnp.zeros_like(base)
 
-    @pl.when(g == 1)
-    def _():
-        total_copy(0, 0, 1).start()
-
     @pl.when(g > 0)
     def _():
-        total_copy(0, 0, 0).wait_recv()
-        base[...] = twofold(tbuf[0])
+        total_copy(0, 0).wait_recv()
+        base[...] = twofold(tbuf[...])
 
     @pl.when(g == 3)
     def _():
@@ -232,17 +234,17 @@
     @pl.when(g == 0)
     def _():
         pl.semaphore_wait(ready.at[0], 1)
-        total_copy(1, 0, 0).start()
-        total_copy(1, 0, 1).wait_recv()
-        tmsg[1] = terms(own + twofold(tbuf[1]))
+        total_copy(1, 0).start()
+        bytes_of(ahead, recv_sem.at[5], False)
+        tmsg[1] = terms(own + sum(twofold(ahead[e]) for e in range(GS)))
         pl.semaphore_wait(ready.at[1], 1)
-        total_copy(3, 1, 0).start()
+        total_copy(3, 1).start()
 
     @pl.when(g == 1)
     def _():
         tmsg[1] = terms(total)
         pl.semaphore_wait(ready.at[0], 1)
-        total_copy(2, 1, 0).start()
+        total_copy(2, 1).start()
 
     def widen(slot, core):
         for b in range(NB):
@@ -289,12 +291,15 @@
     bytes_of(zbuf, send_sem.at[3], True)
     bytes_of(fin.at[pl.ds(0, 15)], send_sem.at[4], True)
 
+    @pl.when(g == 0)
+    def _():
+        total_copy(1, 0).wait_send()
+
     @pl.when(g < 2)
     def _():
-        total_copy(1, 0, 0).wait_send()
-        total_copy(1, 1, 0).wait_send()
-
-    @pl.when(g == 2)
+        total_copy(1, 1).wait_send()
+
+    @pl.when(jnp.logical_not(outer))
     def _():
         bytes_of(nt, send_sem.at[5], True)
 
@@ -315,7 +320,7 @@
             pltpu.VMEM((GS, SLICE, NB * F), jnp.bfloat16),
             pltpu.VMEM((GS, SLICE, NB * F), jnp.bfloat16),
             pltpu.VMEM((2, SLICE, NB * F), jnp.bfloat16),
-            pltpu.VMEM((2, SLICE, NB * F), jnp.bfloat16),
+            pltpu.VMEM((SLICE, NB * F), jnp.bfloat16),
             pltpu.VMEM((SLICE, NB * F), jnp.float32),
             pltpu.VMEM((GS, SLICE, NB * F), jnp.bfloat16),
             pltpu.VMEM((2 * GS, SLICE, NB * F), jnp.bfloat16),
@@ -329,7 +334,7 @@
             pltpu.SemaphoreType.DMA((6,)),
             pltpu.SemaphoreType.DMA((6,)),
             pltpu.SemaphoreType.DMA((NJ - 1,)),
-            pltpu.SemaphoreType.DMA((2,)),
+            pltpu.SemaphoreType.DMA((1,)),
             pltpu.SemaphoreType.DMA((2,)),
             pltpu.SemaphoreType.REGULAR((2,)),
         ],

time: 26.8 us -> 26.2 us (0.978)
  the two profiles are of different devices: /device:TPU:384 before, /device:TPU:256 now
where the time goes in v7:
time: 26.2 us; the launch traced here: 26 us
  Pallas kernels  24.8 us (95%)
  local copies, waits for them, and re-layouts  1.24 us (5%)
    pallas_call x1, Pallas kernels, shards(): pl.pallas_call(kernel, out_shape=jax.ShapeDtypeStruct((NB, SETS), jnp.flo...  24.8 us
    unnamed x1, local copies, waits for them, and re-layouts  1.24 us

profile of v7, /device:TPU:256, one launch (start us, length us, event | category | flops | bytes accessed | tf_op | source)
XLA Modules:
  0.0 26.0 jit_solution(9762449737504979175)
XLA Ops:
  0.0 24.8 %shard_map.91 = f32[2,128]{1,0:T(2,128)} custom-call(bf16[2,64,256]{2,1,0:T(8,128)(2,1)} %normals.1, f32[64,64]{1,0:T(8,128)} %chol.1, f32[1,64]{1,0:T(1,128)} %bitcast.7, f32[1,64]{1,0:T(1,128)} %bitcast.8, f32[64,128]{1,0:T(8,128)} %bmap.1, f32[1,128]{1,0:T(1,128)} %bitcast.9, bf16[128,1024]{1,0:T(8,128)(2,1)} %coef.1, s32[1,1024]{1,0:T(1,128)} %bitcast.5, ...), custom_call_target="tpu_custom_call" | custom-call | tf_op jit(solution)/shard_map/pallas_call | solution.py:312
  24.8 1.2 %copy.11 = f32[2,128]{1,0:T(2,128)} copy(f32[2,128]{1,0:T(2,128)} %shard_map.91) | data formatting | bytes 2048

commit v8 on v7

--- a/solution.py
+++ b/solution.py
@@ -309,6 +309,7 @@
         normals, chol, volatility.reshape(1, -1), start_state.reshape(1, -1), basis_map,
         basis_bias.reshape(1, -1), coef, maturity.reshape(1, -1), netting.reshape(1, -1),
     )
+    args = [pltpu.with_memory_space_constraint(a, pltpu.HBM) for a in args]
     return pl.pallas_call(
         kernel,
         out_shape=jax.ShapeDtypeStruct((NB, SETS), jnp.float32),
@@ -339,7 +340,7 @@
             pltpu.SemaphoreType.REGULAR((2,)),
         ],
         compiler_params=pltpu.CompilerParams(
-            collective_id=0, has_side_effects=True, vmem_limit_bytes=60 << 20
+            collective_id=0, has_side_effects=True, vmem_limit_bytes=24 << 20
         ),
     )(*args)
 

time: 26.2 us -> 24.9 us (0.950)
  local copies, waits for them, and re-layouts: 1.24 us -> 0.56 us
  Pallas kernels: 24.8 us -> 24.2 us
    unnamed x1, local copies, waits for them, and re-layouts: 1.24 us -> 0.56 us
    pallas_call x1, Pallas kernels: 24.8 us -> 24.2 us  [shards(): pl.pallas_call(kernel, out_shape=jax.ShapeDtypeStruct((NB, SETS), jnp.flo...]
where the time goes in v8:
time: 24.9 us; the launch traced here: 24.7 us
  Pallas kernels  24.2 us (97%)
  local copies, waits for them, and re-layouts  0.56 us (2%)
    pallas_call x1, Pallas kernels, shards(): pl.pallas_call(kernel, out_shape=jax.ShapeDtypeStruct((NB, SETS), jnp.flo...  24.2 us
    unnamed x1, local copies, waits for them, and re-layouts  0.56 us

profile of v8, /device:TPU:256, one launch (start us, length us, event | category | flops | bytes accessed | tf_op | source)
XLA Modules:
  0.0 24.7 jit_solution(13238506753990585947)
XLA Ops:
  0.0 24.2 %shard_map.91 = f32[2,128]{1,0:T(2,128)S(1)} custom-call(bf16[2,64,256]{2,1,0:T(8,128)(2,1)} %normals.1, f32[64,64]{1,0:T(8,128)} %chol.1, f32[1,64]{1,0:T(1,128)} %bitcast.7, f32[1,64]{1,0:T(1,128)} %bitcast.8, f32[64,128]{1,0:T(8,128)} %bmap.1, f32[1,128]{1,0:T(1,128)} %bitcast.9, bf16[128,1024]{1,0:T(8,128)(2,1)} %coef.1, s32[1,1024]{1,0:T(1,128)} %bitcast.5, ...), custom_call_target="tpu_custom_call" | custom-call | tf_op jit(solution)/shard_map/pallas_call | solution.py:313
  24.2 0.6 %copy.11 = f32[2,128]{1,0:T(2,128)} copy(f32[2,128]{1,0:T(2,128)S(1)} %shard_map.91) | data formatting | bytes 2048

commit v9 on v8

--- a/solution.py
+++ b/solution.py
@@ -99,6 +99,38 @@
     flat = v_norm[...].reshape(NB * F, GS * SLICE).astype(jnp.float32)
     nt[...] = flat.T.astype(jnp.bfloat16).reshape(GS, SLICE, NB * F)
 
+    heard = jnp.where(g == 0, 0, 1) + jnp.where(outer, 0, GS)
+    pl.semaphore_wait(barrier, GS + 4 + 3 + heard)
+
+    for i in (2, 3, 1, 0):
+        pltpu.make_async_remote_copy(
+            src_ref=nt.at[lax.rem(w + i, GS)], dst_ref=arrived.at[w], send_sem=send_sem.at[0], recv_sem=recv_sem.at[0],
+            device_id=mate(i), device_id_type=MESH,
+        ).start()
+
+    @pl.when(jnp.logical_not(outer))
+    def _():
+        for i in range(GS):
+            pltpu.make_async_remote_copy(
+                src_ref=nt.at[lax.rem(w + i, GS)], dst_ref=ahead.at[w], send_sem=send_sem.at[5], recv_sem=recv_sem.at[5],
+                device_id=across(i), device_id_type=MESH,
+            ).start()
+
+    def say_ready(to, slot):
+        pl.semaphore_signal(ready.at[slot], inc=1, device_id=counterpart(to), device_id_type=MESH)
+
+    @pl.when(g == 1)
+    def _():
+        say_ready(0, 0)
+
+    @pl.when(g == 2)
+    def _():
+        say_ready(1, 0)
+
+    @pl.when(g == 3)
+    def _():
+        say_ready(0, 1)
+
     for load in loads[1:4]:
         load.wait()
     local_set = v_net[...] - t * SETS
@@ -113,38 +145,6 @@
         largest = jnp.maximum(jnp.max(jnp.abs(folded), axis=0, keepdims=True), np.float32(1e-30))
         unit[b : b + 1, :] = largest * np.float32(1.0 / TOP)
         cbuf[0, c, b] = jnp.round(folded * (np.float32(TOP) / largest)).astype(jnp.int32).astype(jnp.int16)
-
-    heard = jnp.where(g == 0, 0, 1) + jnp.where(outer, 0, GS)
-    pl.semaphore_wait(barrier, GS + 4 + 3 + heard)
-
-    for i in (2, 3, 1, 0):
-        pltpu.make_async_remote_copy(
-            src_ref=nt.at[lax.rem(w + i, GS)], dst_ref=arrived.at[w], send_sem=send_sem.at[0], recv_sem=recv_sem.at[0],
-            device_id=mate(i), device_id_type=MESH,
-        ).start()
-
-    @pl.when(jnp.logical_not(outer))
-    def _():
-        for i in range(GS):
-            pltpu.make_async_remote_copy(
-                src_ref=nt.at[lax.rem(w + i, GS)], dst_ref=ahead.at[w], send_sem=send_sem.at[5], recv_sem=recv_sem.at[5],
-                device_id=across(i), device_id_type=MESH,
-            ).start()
-
-    def say_ready(to, slot):
-        pl.semaphore_signal(ready.at[slot], inc=1, device_id=counterpart(to), device_id_type=MESH)
-
-    @pl.when(g == 1)
-    def _():
-        say_ready(0, 0)
-
-    @pl.when(g == 2)
-    def _():
-        say_ready(1, 0)
-
-    @pl.when(g == 3)
-    def _():
-        say_ready(0, 1)
 
     c_copies = [
         pltpu.make_async_remote_copy(
@@ -194,7 +194,9 @@
         high = value.astype(jnp.bfloat16).astype(jnp.float32)
         return jnp.where(later_half, value - high, value).astype(jnp.bfloat16)
 
-    own = sum(twofold(arrived[e]) for e in range(GS))
+    blocks = [arrived[e].astype(jnp.float32) for e in range(GS)]
+    pairs = [block + pltpu.roll(block, F, axis=1) for block in blocks]
+    own = pairs[0] + pairs[1] + pairs[2] + pairs[3]
     tmsg[0] = terms(own)
 
     def total_copy(to, message):
@@ -206,12 +208,20 @@
     @pl.when(g == 0)
     def _():
         base[...] = jnp.zeros_like(base)
+        pl.semaphore_wait(ready.at[0], 1)
+        total_copy(1, 0).start()
 
     @pl.when(g > 0)
     def _():
         total_copy(0, 0).wait_recv()
         base[...] = twofold(tbuf[...])
 
+    @pl.when(g == 1)
+    def _():
+        tmsg[1] = terms(own + base[...])
+        pl.semaphore_wait(ready.at[0], 1)
+        total_copy(2, 1).start()
+
     @pl.when(g == 3)
     def _():
         bytes_of(ahead, recv_sem.at[5], False)
@@ -219,32 +229,20 @@
 
     total = base[...]
     for e in range(GS):
-        block = arrived[e].astype(jnp.float32)
-        pair = block + pltpu.roll(block, F, axis=1)
-        sums[e] = (total + jnp.where(later_half, pair, block)).astype(jnp.bfloat16)
-        total = total + pair
-
-    for i in (2, 3, 1, 0):
+        sums[e] = (total + jnp.where(later_half, pairs[e], blocks[e])).astype(jnp.bfloat16)
+        total = total + pairs[e]
         for where in (twin, t):
             pltpu.make_async_remote_copy(
-                src_ref=sums.at[lax.rem(w + i, GS)], dst_ref=zbuf.at[par * GS + w], send_sem=send_sem.at[3], recv_sem=recv_sem.at[3],
-                device_id={**mate(i), "trade": where}, device_id_type=MESH,
+                src_ref=sums.at[e], dst_ref=zbuf.at[par * GS + w], send_sem=send_sem.at[3], recv_sem=recv_sem.at[3],
+                device_id={"date": g * GS + e, "path": p1, "trade": where}, device_id_type=MESH,
             ).start()
 
     @pl.when(g == 0)
     def _():
-        pl.semaphore_wait(ready.at[0], 1)
-        total_copy(1, 0).start()
         bytes_of(ahead, recv_sem.at[5], False)
         tmsg[1] = terms(own + sum(twofold(ahead[e]) for e in range(GS)))
         pl.semaphore_wait(ready.at[1], 1)
         total_copy(3, 1).start()
-
-    @pl.when(g == 1)
-    def _():
-        tmsg[1] = terms(total)
-        pl.semaphore_wait(ready.at[0], 1)
-        total_copy(2, 1).start()
 
     def widen(slot, core):
         for b in range(NB):

time: 24.9 us -> 24.6 us (0.988)
  the two profiles are of different devices: /device:TPU:256 before, /device:TPU:320 now
where the time goes in v9:
time: 24.6 us; the launch traced here: 24.5 us
  Pallas kernels  23.9 us (97%)
  local copies, waits for them, and re-layouts  0.56 us (2%)
    pallas_call x1, Pallas kernels, shards(): pl.pallas_call(kernel, out_shape=jax.ShapeDtypeStruct((NB, SETS), jnp.flo...  23.9 us
    unnamed x1, local copies, waits for them, and re-layouts  0.56 us

profile of v9, /device:TPU:320, one launch (start us, length us, event | category | flops | bytes accessed | tf_op | source)
XLA Modules:
  0.0 24.5 jit_solution(9494904302937537291)
XLA Ops:
  0.0 23.9 %shard_map.91 = f32[2,128]{1,0:T(2,128)S(1)} custom-call(bf16[2,64,256]{2,1,0:T(8,128)(2,1)} %normals.1, f32[64,64]{1,0:T(8,128)} %chol.1, f32[1,64]{1,0:T(1,128)} %bitcast.7, f32[1,64]{1,0:T(1,128)} %bitcast.8, f32[64,128]{1,0:T(8,128)} %bmap.1, f32[1,128]{1,0:T(1,128)} %bitcast.9, bf16[128,1024]{1,0:T(8,128)(2,1)} %coef.1, s32[1,1024]{1,0:T(1,128)} %bitcast.5, ...), custom_call_target="tpu_custom_call" | custom-call | tf_op jit(solution)/shard_map/pallas_call | solution.py:311
  23.9 0.6 %copy.11 = f32[2,128]{1,0:T(2,128)} copy(f32[2,128]{1,0:T(2,128)S(1)} %shard_map.91) | data formatting | bytes 2048

commit v10 on v9

--- a/solution.py
+++ b/solution.py
@@ -14,6 +14,8 @@
 SETS = 128
 GS = 4
 SLICE = 64
+HALF = SLICE // 2
+PATHS = GS * SLICE
 TOP = 127 * 256
 NJ = 4
 HIGH = lax.Precision.HIGHEST
@@ -23,7 +25,7 @@
     normals, chol, vol, start, bmap, bias, coef, mat, net,
     out,
     v_norm, v_chol, v_vol, v_start, v_bmap, v_bias, v_coef, v_mat, v_net,
-    nt, arrived, ahead, tmsg, tbuf, base, sums, zbuf, cbuf, cwide, unit, wbuf, part, fin,
+    own_n, near_n, local, slices, arrived, ahead, tmsg, tbuf, base, sums, zbuf, zrows, cbuf, cwide, unit, wbuf, part, fin,
     load_sem, send_sem, recv_sem, c_sem, t_sem, t_sent, ready,
 ):
     d, t, p = lax.axis_index("date"), lax.axis_index("trade"), lax.axis_index("path")
@@ -95,16 +97,27 @@
     for load in loads:
         load.start()
 
+    def odd_half(rows):
+        return lax.broadcasted_iota(jnp.int32, (rows, NB * F), 1) >= F
+
+    def swapped(block):
+        return pltpu.roll(block, F, axis=1)
+
     loads[0].wait()
-    flat = v_norm[...].reshape(NB * F, GS * SLICE).astype(jnp.float32)
-    nt[...] = flat.T.astype(jnp.bfloat16).reshape(GS, SLICE, NB * F)
+    normal = v_norm[...].reshape(NB * F, PATHS).astype(jnp.float32).T
+    both = normal + swapped(normal)
+    for i in range(GS):
+        first = i * SLICE
+        slices[i] = jnp.where(
+            odd_half(HALF), both[first + HALF : first + SLICE], both[first : first + HALF]
+        ).astype(jnp.bfloat16)
 
     heard = jnp.where(g == 0, 0, 1) + jnp.where(outer, 0, GS)
     pl.semaphore_wait(barrier, GS + 4 + 3 + heard)
 
     for i in (2, 3, 1, 0):
         pltpu.make_async_remote_copy(
-            src_ref=nt.at[lax.rem(w + i, GS)], dst_ref=arrived.at[w], send_sem=send_sem.at[0], recv_sem=recv_sem.at[0],
+            src_ref=slices.at[lax.rem(w + i, GS)], dst_ref=arrived.at[w], send_sem=send_sem.at[0], recv_sem=recv_sem.at[0],
             device_id=mate(i), device_id_type=MESH,
         ).start()
 
@@ -112,7 +125,7 @@
     def _():
         for i in range(GS):
             pltpu.make_async_remote_copy(
-                src_ref=nt.at[lax.rem(w + i, GS)], dst_ref=ahead.at[w], send_sem=send_sem.at[5], recv_sem=recv_sem.at[5],
+                src_ref=slices.at[lax.rem(w + i, GS)], dst_ref=ahead.at[w], send_sem=send_sem.at[5], recv_sem=recv_sem.at[5],
                 device_id=across(i), device_id_type=MESH,
             ).start()
 
@@ -130,6 +143,14 @@
     @pl.when(g == 3)
     def _():
         say_ready(0, 1)
+
+    own_n[...] = normal.astype(jnp.bfloat16)
+    neighbour = pltpu.make_async_remote_copy(
+        src_ref=own_n, dst_ref=near_n, send_sem=send_sem.at[6], recv_sem=recv_sem.at[6],
+        device_id={"trade": twin}, device_id_type=MESH,
+    )
+    neighbour.start()
+    local[par] = jnp.where(odd_half(PATHS), both, normal)
 
     for load in loads[1:4]:
         load.wait()
@@ -184,20 +205,9 @@
         return whole.wait_send() if send else whole.wait_recv()
 
     bytes_of(arrived, recv_sem.at[0], False)
-    later_half = lax.broadcasted_iota(jnp.int32, (SLICE, NB * F), 1) >= F
-
-    def twofold(message):
-        message = message.astype(jnp.float32)
-        return message + pltpu.roll(message, F, axis=1)
-
-    def terms(value):
-        high = value.astype(jnp.bfloat16).astype(jnp.float32)
-        return jnp.where(later_half, value - high, value).astype(jnp.bfloat16)
-
     blocks = [arrived[e].astype(jnp.float32) for e in range(GS)]
-    pairs = [block + pltpu.roll(block, F, axis=1) for block in blocks]
-    own = pairs[0] + pairs[1] + pairs[2] + pairs[3]
-    tmsg[0] = terms(own)
+    own = blocks[0] + blocks[1] + blocks[2] + blocks[3]
+    tmsg[0] = own.astype(jnp.bfloat16)
 
     def total_copy(to, message):
         return pltpu.make_async_remote_copy(
@@ -214,23 +224,23 @@
     @pl.when(g > 0)
     def _():
         total_copy(0, 0).wait_recv()
-        base[...] = twofold(tbuf[...])
+        base[...] = tbuf[...].astype(jnp.float32)
 
     @pl.when(g == 1)
     def _():
-        tmsg[1] = terms(own + base[...])
+        tmsg[1] = (own + base[...]).astype(jnp.bfloat16)
         pl.semaphore_wait(ready.at[0], 1)
         total_copy(2, 1).start()
 
     @pl.when(g == 3)
     def _():
         bytes_of(ahead, recv_sem.at[5], False)
-        base[...] += sum(twofold(ahead[e]) for e in range(GS))
+        base[...] += sum(ahead[e].astype(jnp.float32) for e in range(GS))
 
     total = base[...]
     for e in range(GS):
-        sums[e] = (total + jnp.where(later_half, pairs[e], blocks[e])).astype(jnp.bfloat16)
-        total = total + pairs[e]
+        sums[e] = total.astype(jnp.bfloat16)
+        total = total + blocks[e]
         for where in (twin, t):
             pltpu.make_async_remote_copy(
                 src_ref=sums.at[e], dst_ref=zbuf.at[par * GS + w], send_sem=send_sem.at[3], recv_sem=recv_sem.at[3],
@@ -240,9 +250,13 @@
     @pl.when(g == 0)
     def _():
         bytes_of(ahead, recv_sem.at[5], False)
-        tmsg[1] = terms(own + sum(twofold(ahead[e]) for e in range(GS)))
+        tmsg[1] = (own + sum(ahead[e].astype(jnp.float32) for e in range(GS))).astype(jnp.bfloat16)
         pl.semaphore_wait(ready.at[1], 1)
         total_copy(3, 1).start()
+
+    neighbour.wait_recv()
+    normal = near_n[...].astype(jnp.float32)
+    local[1 - par] = normal + jnp.where(odd_half(PATHS), swapped(normal), 0.0)
 
     def widen(slot, core):
         for b in range(NB):
@@ -261,7 +275,15 @@
         widen(slot, c1)
 
     bytes_of(zbuf, recv_sem.at[3], False)
-    z = zbuf[...].reshape(2 * GS * SLICE, NB * F)
+    for half in range(2):
+        for i in range(GS):
+            before = zbuf[half * GS + i].astype(jnp.float32)
+            across_lanes = swapped(before)
+            rows = pl.ds(i * SLICE, HALF)
+            zrows[half, rows] = (local[half, rows] + jnp.where(odd_half(HALF), across_lanes, before)).astype(jnp.bfloat16)
+            rows = pl.ds(i * SLICE + HALF, HALF)
+            zrows[half, rows] = (local[half, rows] + jnp.where(odd_half(HALF), before, across_lanes)).astype(jnp.bfloat16)
+    z = zrows[...].reshape(2 * PATHS, NB * F)
     pre = jnp.dot(jnp.concatenate([z, z], axis=1), wbuf[...], preferred_element_type=jnp.float32)
     basis = jnp.tanh(pre + offsets).astype(jnp.bfloat16)
     twice = [jnp.concatenate([basis[:, b * K : (b + 1) * K]] * 2, axis=1) for b in range(NB)]
@@ -281,9 +303,10 @@
 
     fin[c * 2 + p] = part[0, c]
     bytes_of(fin.at[pl.ds(0, 15)], recv_sem.at[4], False)
-    out[...] = jnp.sum(fin[...], axis=0) * unit[...] * np.float32(1.0 / (GS * SLICE * 32))
-
-    bytes_of(nt, send_sem.at[0], True)
+    out[...] = jnp.sum(fin[...], axis=0) * unit[...] * np.float32(1.0 / (PATHS * 32))
+
+    bytes_of(slices, send_sem.at[0], True)
+    neighbour.wait_send()
     bytes_of(cbuf.at[pl.ds(0, NJ - 1), c], send_sem.at[1], True)
     bytes_of(cbuf.at[:, c], send_sem.at[2], True)
     bytes_of(zbuf, send_sem.at[3], True)
@@ -299,7 +322,7 @@
 
     @pl.when(jnp.logical_not(outer))
     def _():
-        bytes_of(nt, send_sem.at[5], True)
+        bytes_of(slices, send_sem.at[5], True)
 
 
 def shards(normals, chol, volatility, start_state, basis_map, basis_bias, coef, maturity, netting):
@@ -315,14 +338,18 @@
         out_specs=pl.BlockSpec(memory_space=pltpu.VMEM),
         scratch_shapes=[pltpu.VMEM(a.shape, a.dtype) for a in args]
         + [
-            pltpu.VMEM((GS, SLICE, NB * F), jnp.bfloat16),
-            pltpu.VMEM((GS, SLICE, NB * F), jnp.bfloat16),
-            pltpu.VMEM((GS, SLICE, NB * F), jnp.bfloat16),
-            pltpu.VMEM((2, SLICE, NB * F), jnp.bfloat16),
-            pltpu.VMEM((SLICE, NB * F), jnp.bfloat16),
-            pltpu.VMEM((SLICE, NB * F), jnp.float32),
-            pltpu.VMEM((GS, SLICE, NB * F), jnp.bfloat16),
-            pltpu.VMEM((2 * GS, SLICE, NB * F), jnp.bfloat16),
+            pltpu.VMEM((PATHS, NB * F), jnp.bfloat16),
+            pltpu.VMEM((PATHS, NB * F), jnp.bfloat16),
+            pltpu.VMEM((2, PATHS, NB * F), jnp.float32),
+            pltpu.VMEM((GS, HALF, NB * F), jnp.bfloat16),
+            pltpu.VMEM((GS, HALF, NB * F), jnp.bfloat16),
+            pltpu.VMEM((GS, HALF, NB * F), jnp.bfloat16),
+            pltpu.VMEM((2, HALF, NB * F), jnp.bfloat16),
+            pltpu.VMEM((HALF, NB * F), jnp.bfloat16),
+            pltpu.VMEM((HALF, NB * F), jnp.float32),
+            pltpu.VMEM((GS, HALF, NB * F), jnp.bfloat16),
+            pltpu.VMEM((2 * GS, HALF, NB * F), jnp.bfloat16),
+            pltpu.VMEM((2, PATHS, NB * F), jnp.bfloat16),
             pltpu.VMEM((NJ, 2, NB, K, SETS), jnp.int16),
             pltpu.VMEM((NJ, 2, NB, 2 * K, SETS), jnp.bfloat16),
             pltpu.VMEM((NB, SETS), jnp.float32),
@@ -330,8 +357,8 @@
             pltpu.VMEM((NJ, 2, NB, SETS), jnp.float32),
             pltpu.VMEM((16, NB, SETS), jnp.float32),
             pltpu.SemaphoreType.DMA((len(args),)),
-            pltpu.SemaphoreType.DMA((6,)),
-            pltpu.SemaphoreType.DMA((6,)),
+            pltpu.SemaphoreType.DMA((7,)),
+            pltpu.SemaphoreType.DMA((7,)),
             pltpu.SemaphoreType.DMA((NJ - 1,)),
             pltpu.SemaphoreType.DMA((1,)),
             pltpu.SemaphoreType.DMA((2,)),

time: 24.6 us -> 24.3 us (0.988)
  the two profiles are of different devices: /device:TPU:320 before, /device:TPU:1 now
where the time goes in v10:
time: 24.3 us; the launch traced here: 24 us
  Pallas kernels  23.5 us (97%)
  local copies, waits for them, and re-layouts  0.56 us (2%)
    pallas_call x1, Pallas kernels, shards(): pl.pallas_call(kernel, out_shape=jax.ShapeDtypeStruct((NB, SETS), jnp.flo...  23.5 us
    unnamed x1, local copies, waits for them, and re-layouts  0.56 us

profile of v10, /device:TPU:1, one launch (start us, length us, event | category | flops | bytes accessed | tf_op | source)
XLA Modules:
  0.0 24.0 jit_solution(12873515868393249524)
XLA Ops:
  0.0 23.5 %shard_map.91 = f32[2,128]{1,0:T(2,128)S(1)} custom-call(bf16[2,64,256]{2,1,0:T(8,128)(2,1)} %normals.1, f32[64,64]{1,0:T(8,128)} %chol.1, f32[1,64]{1,0:T(1,128)} %bitcast.7, f32[1,64]{1,0:T(1,128)} %bitcast.8, f32[64,128]{1,0:T(8,128)} %bmap.1, f32[1,128]{1,0:T(1,128)} %bitcast.9, bf16[128,1024]{1,0:T(8,128)(2,1)} %coef.1, s32[1,1024]{1,0:T(1,128)} %bitcast.5, ...), custom_call_target="tpu_custom_call" | custom-call | tf_op jit(solution)/shard_map/pallas_call | solution.py:334
  23.5 0.6 %copy.11 = f32[2,128]{1,0:T(2,128)} copy(f32[2,128]{1,0:T(2,128)S(1)} %shard_map.91) | data formatting | bytes 2048

commit v11 on v10

--- a/solution.py
+++ b/solution.py
@@ -25,7 +25,7 @@
     normals, chol, vol, start, bmap, bias, coef, mat, net,
     out,
     v_norm, v_chol, v_vol, v_start, v_bmap, v_bias, v_coef, v_mat, v_net,
-    own_n, near_n, local, slices, arrived, ahead, tmsg, tbuf, base, sums, zbuf, zrows, cbuf, cwide, unit, wbuf, part, fin,
+    own_n, near_n, local, slices, arrived, ahead, tmsg, tbuf, base, sums, zbuf, tz, zrows, cbuf, cwide, unit, wbuf, part, fin,
     load_sem, send_sem, recv_sem, c_sem, t_sem, t_sent, ready,
 ):
     d, t, p = lax.axis_index("date"), lax.axis_index("trade"), lax.axis_index("path")
@@ -53,8 +53,8 @@
     def mate(i):
         return {"date": g * GS + lax.rem(w + i, GS), "path": p1}
 
-    def counterpart(group):
-        return {"date": group * GS + w}
+    def counterpart(group, where=t):
+        return {"date": group * GS + w, "trade": where}
 
     for i in range(GS):
         hello(mate(i))
@@ -73,6 +73,7 @@
     @pl.when(g == 1)
     def _():
         hello(counterpart(2))
+        hello(counterpart(2, twin))
 
     outer = jnp.logical_or(g == 0, g == 3)
     beside = jnp.where(g < 2, 1 - g, 5 - g)
@@ -112,7 +113,7 @@
             odd_half(HALF), both[first + HALF : first + SLICE], both[first : first + HALF]
         ).astype(jnp.bfloat16)
 
-    heard = jnp.where(g == 0, 0, 1) + jnp.where(outer, 0, GS)
+    heard = jnp.where(g == 0, 0, 1) + jnp.where(g == 2, 1, 0) + jnp.where(outer, 0, GS)
     pl.semaphore_wait(barrier, GS + 4 + 3 + heard)
 
     for i in (2, 3, 1, 0):
@@ -129,8 +130,8 @@
                 device_id=across(i), device_id_type=MESH,
             ).start()
 
-    def say_ready(to, slot):
-        pl.semaphore_signal(ready.at[slot], inc=1, device_id=counterpart(to), device_id_type=MESH)
+    def say_ready(to, slot, where=t):
+        pl.semaphore_signal(ready.at[slot], inc=1, device_id=counterpart(to, where), device_id_type=MESH)
 
     @pl.when(g == 1)
     def _():
@@ -139,6 +140,7 @@
     @pl.when(g == 2)
     def _():
         say_ready(1, 0)
+        say_ready(1, 0, twin)
 
     @pl.when(g == 3)
     def _():
@@ -221,16 +223,14 @@
         pl.semaphore_wait(ready.at[0], 1)
         total_copy(1, 0).start()
 
-    @pl.when(g > 0)
+    @pl.when(g == 2)
+    def _():
+        base[...] = jnp.zeros_like(base)
+
+    @pl.when(jnp.logical_or(g == 1, g == 3))
     def _():
         total_copy(0, 0).wait_recv()
         base[...] = tbuf[...].astype(jnp.float32)
-
-    @pl.when(g == 1)
-    def _():
-        tmsg[1] = (own + base[...]).astype(jnp.bfloat16)
-        pl.semaphore_wait(ready.at[0], 1)
-        total_copy(2, 1).start()
 
     @pl.when(g == 3)
     def _():
@@ -247,6 +247,17 @@
                 device_id={"date": g * GS + e, "path": p1, "trade": where}, device_id_type=MESH,
             ).start()
 
+    @pl.when(g == 1)
+    def _():
+        tmsg[1] = (own + base[...]).astype(jnp.bfloat16)
+        pl.semaphore_wait(ready.at[0], 2)
+        for i in range(GS):
+            for where in (twin, t):
+                pltpu.make_async_remote_copy(
+                    src_ref=tmsg.at[1], dst_ref=tz.at[par * GS + w], send_sem=t_sent.at[1], recv_sem=t_sem.at[1],
+                    device_id={"date": 2 * GS + i, "path": p1, "trade": where}, device_id_type=MESH,
+                ).start()
+
     @pl.when(g == 0)
     def _():
         bytes_of(ahead, recv_sem.at[5], False)
@@ -274,15 +285,26 @@
     for slot in range(NJ):
         widen(slot, c1)
 
+    def unpacked(packed):
+        packed = packed.astype(jnp.float32)
+        other_half = swapped(packed)
+        return jnp.where(odd_half(HALF), other_half, packed), jnp.where(odd_half(HALF), packed, other_half)
+
+    @pl.when(g == 2)
+    def _():
+        bytes_of(tz, t_sem.at[1], False)
+        for half in range(2):
+            for i in range(GS):
+                first, last = unpacked(tz[half * GS + i])
+                local[half, pl.ds(i * SLICE, HALF)] += first
+                local[half, pl.ds(i * SLICE + HALF, HALF)] += last
+
     bytes_of(zbuf, recv_sem.at[3], False)
     for half in range(2):
         for i in range(GS):
-            before = zbuf[half * GS + i].astype(jnp.float32)
-            across_lanes = swapped(before)
-            rows = pl.ds(i * SLICE, HALF)
-            zrows[half, rows] = (local[half, rows] + jnp.where(odd_half(HALF), across_lanes, before)).astype(jnp.bfloat16)
-            rows = pl.ds(i * SLICE + HALF, HALF)
-            zrows[half, rows] = (local[half, rows] + jnp.where(odd_half(HALF), before, across_lanes)).astype(jnp.bfloat16)
+            first, last = unpacked(zbuf[half * GS + i])
+            zrows[half, pl.ds(i * SLICE, HALF)] = (local[half, pl.ds(i * SLICE, HALF)] + first).astype(jnp.bfloat16)
+            zrows[half, pl.ds(i * SLICE + HALF, HALF)] = (local[half, pl.ds(i * SLICE + HALF, HALF)] + last).astype(jnp.bfloat16)
     z = zrows[...].reshape(2 * PATHS, NB * F)
     pre = jnp.dot(jnp.concatenate([z, z], axis=1), wbuf[...], preferred_element_type=jnp.float32)
     basis = jnp.tanh(pre + offsets).astype(jnp.bfloat16)
@@ -316,9 +338,13 @@
     def _():
         total_copy(1, 0).wait_send()
 
-    @pl.when(g < 2)
+    @pl.when(g == 0)
     def _():
         total_copy(1, 1).wait_send()
+
+    @pl.when(g == 1)
+    def _():
+        bytes_of(tz, t_sent.at[1], True)
 
     @pl.when(jnp.logical_not(outer))
     def _():
@@ -349,6 +375,7 @@
             pltpu.VMEM((HALF, NB * F), jnp.float32),
             pltpu.VMEM((GS, HALF, NB * F), jnp.bfloat16),
             pltpu.VMEM((2 * GS, HALF, NB * F), jnp.bfloat16),
+            pltpu.VMEM((2 * GS, HALF, NB * F), jnp.bfloat16),
             pltpu.VMEM((2, PATHS, NB * F), jnp.bfloat16),
             pltpu.VMEM((NJ, 2, NB, K, SETS), jnp.int16),
             pltpu.VMEM((NJ, 2, NB, 2 * K, SETS), jnp.bfloat16),
@@ -360,7 +387,7 @@
             pltpu.SemaphoreType.DMA((7,)),
             pltpu.SemaphoreType.DMA((7,)),
             pltpu.SemaphoreType.DMA((NJ - 1,)),
-            pltpu.SemaphoreType.DMA((1,)),
+            pltpu.SemaphoreType.DMA((2,)),
             pltpu.SemaphoreType.DMA((2,)),
             pltpu.SemaphoreType.REGULAR((2,)),
         ],

time: 24.3 us -> 24.2 us (level)
  no operation moved by 1% of the time
where the time goes in v11:
time: 24.2 us; the launch traced here: 24 us
  Pallas kernels  23.5 us (97%)
  local copies, waits for them, and re-layouts  0.56 us (2%)
    pallas_call x1, Pallas kernels, shards(): pl.pallas_call(kernel, out_shape=jax.ShapeDtypeStruct((NB, SETS), jnp.flo...  23.5 us
    unnamed x1, local copies, waits for them, and re-layouts  0.56 us

profile of v11, /device:TPU:1, one launch (start us, length us, event | category | flops | bytes accessed | tf_op | source)
XLA Modules:
  0.0 24.0 jit_solution(16099793195236331918)
XLA Ops:
  0.0 23.5 %shard_map.91 = f32[2,128]{1,0:T(2,128)S(1)} custom-call(bf16[2,64,256]{2,1,0:T(8,128)(2,1)} %normals.1, f32[64,64]{1,0:T(8,128)} %chol.1, f32[1,64]{1,0:T(1,128)} %bitcast.7, f32[1,64]{1,0:T(1,128)} %bitcast.8, f32[64,128]{1,0:T(8,128)} %bmap.1, f32[1,128]{1,0:T(1,128)} %bitcast.9, bf16[128,1024]{1,0:T(8,128)(2,1)} %coef.1, s32[1,1024]{1,0:T(1,128)} %bitcast.5, ...), custom_call_target="tpu_custom_call" | custom-call | tf_op jit(solution)/shard_map/pallas_call | solution.py:360
  23.5 0.6 %copy.11 = f32[2,128]{1,0:T(2,128)} copy(f32[2,128]{1,0:T(2,128)S(1)} %shard_map.91) | data formatting | bytes 2048

commit v12 on v11

--- a/solution.py
+++ b/solution.py
@@ -113,47 +113,6 @@
             odd_half(HALF), both[first + HALF : first + SLICE], both[first : first + HALF]
         ).astype(jnp.bfloat16)
 
-    heard = jnp.where(g == 0, 0, 1) + jnp.where(g == 2, 1, 0) + jnp.where(outer, 0, GS)
-    pl.semaphore_wait(barrier, GS + 4 + 3 + heard)
-
-    for i in (2, 3, 1, 0):
-        pltpu.make_async_remote_copy(
-            src_ref=slices.at[lax.rem(w + i, GS)], dst_ref=arrived.at[w], send_sem=send_sem.at[0], recv_sem=recv_sem.at[0],
-            device_id=mate(i), device_id_type=MESH,
-        ).start()
-
-    @pl.when(jnp.logical_not(outer))
-    def _():
-        for i in range(GS):
-            pltpu.make_async_remote_copy(
-                src_ref=slices.at[lax.rem(w + i, GS)], dst_ref=ahead.at[w], send_sem=send_sem.at[5], recv_sem=recv_sem.at[5],
-                device_id=across(i), device_id_type=MESH,
-            ).start()
-
-    def say_ready(to, slot, where=t):
-        pl.semaphore_signal(ready.at[slot], inc=1, device_id=counterpart(to, where), device_id_type=MESH)
-
-    @pl.when(g == 1)
-    def _():
-        say_ready(0, 0)
-
-    @pl.when(g == 2)
-    def _():
-        say_ready(1, 0)
-        say_ready(1, 0, twin)
-
-    @pl.when(g == 3)
-    def _():
-        say_ready(0, 1)
-
-    own_n[...] = normal.astype(jnp.bfloat16)
-    neighbour = pltpu.make_async_remote_copy(
-        src_ref=own_n, dst_ref=near_n, send_sem=send_sem.at[6], recv_sem=recv_sem.at[6],
-        device_id={"trade": twin}, device_id_type=MESH,
-    )
-    neighbour.start()
-    local[par] = jnp.where(odd_half(PATHS), both, normal)
-
     for load in loads[1:4]:
         load.wait()
     local_set = v_net[...] - t * SETS
@@ -168,6 +127,47 @@
         largest = jnp.maximum(jnp.max(jnp.abs(folded), axis=0, keepdims=True), np.float32(1e-30))
         unit[b : b + 1, :] = largest * np.float32(1.0 / TOP)
         cbuf[0, c, b] = jnp.round(folded * (np.float32(TOP) / largest)).astype(jnp.int32).astype(jnp.int16)
+
+    heard = jnp.where(g == 0, 0, 1) + jnp.where(g == 2, 1, 0) + jnp.where(outer, 0, GS)
+    pl.semaphore_wait(barrier, GS + 4 + 3 + heard)
+
+    for i in (2, 3, 1, 0):
+        pltpu.make_async_remote_copy(
+            src_ref=slices.at[lax.rem(w + i, GS)], dst_ref=arrived.at[w], send_sem=send_sem.at[0], recv_sem=recv_sem.at[0],
+            device_id=mate(i), device_id_type=MESH,
+        ).start()
+
+    @pl.when(jnp.logical_not(outer))
+    def _():
+        for i in range(GS):
+            pltpu.make_async_remote_copy(
+                src_ref=slices.at[lax.rem(w + i, GS)], dst_ref=ahead.at[w], send_sem=send_sem.at[5], recv_sem=recv_sem.at[5],
+                device_id=across(i), device_id_type=MESH,
+            ).start()
+
+    def say_ready(to, slot, where=t):
+        pl.semaphore_signal(ready.at[slot], inc=1, device_id=counterpart(to, where), device_id_type=MESH)
+
+    @pl.when(g == 1)
+    def _():
+        say_ready(0, 0)
+
+    @pl.when(g == 2)
+    def _():
+        say_ready(1, 0)
+        say_ready(1, 0, twin)
+
+    @pl.when(g == 3)
+    def _():
+        say_ready(0, 1)
+
+    own_n[...] = normal.astype(jnp.bfloat16)
+    neighbour = pltpu.make_async_remote_copy(
+        src_ref=own_n, dst_ref=near_n, send_sem=send_sem.at[6], recv_sem=recv_sem.at[6],
+        device_id={"trade": twin}, device_id_type=MESH,
+    )
+    neighbour.start()
+    local[par] = jnp.where(odd_half(PATHS), both, normal)
 
     c_copies = [
         pltpu.make_async_remote_copy(
@@ -281,9 +281,6 @@
         c_copies[slot - 1].wait_recv()
         pass_on(slot).start()
         widen(slot, c)
-    bytes_of(cbuf.at[:, c1], recv_sem.at[2], False)
-    for slot in range(NJ):
-        widen(slot, c1)
 
     def unpacked(packed):
         packed = packed.astype(jnp.float32)
@@ -309,6 +306,10 @@
     pre = jnp.dot(jnp.concatenate([z, z], axis=1), wbuf[...], preferred_element_type=jnp.float32)
     basis = jnp.tanh(pre + offsets).astype(jnp.bfloat16)
     twice = [jnp.concatenate([basis[:, b * K : (b + 1) * K]] * 2, axis=1) for b in range(NB)]
+
+    bytes_of(cbuf.at[:, c1], recv_sem.at[2], False)
+    for slot in range(NJ):
+        widen(slot, c1)
 
     for slot in range(NJ - 1, -1, -1):
         for b in range(NB):

time: 24.2 us -> 24 us (level)
  no operation moved by 1% of the time
where the time goes in v12:
time: 24 us; the launch traced here: 23.9 us
  Pallas kernels  23.4 us (98%)
  local copies, waits for them, and re-layouts  0.56 us (2%)
    pallas_call x1, Pallas kernels, shards(): pl.pallas_call(kernel, out_shape=jax.ShapeDtypeStruct((NB, SETS), jnp.flo...  23.4 us
    unnamed x1, local copies, waits for them, and re-layouts  0.56 us

profile of v12, /device:TPU:1, one launch (start us, length us, event | category | flops | bytes accessed | tf_op | source)
XLA Modules:
  0.0 23.9 jit_solution(9219021886003983716)
XLA Ops:
  0.0 23.4 %shard_map.91 = f32[2,128]{1,0:T(2,128)S(1)} custom-call(bf16[2,64,256]{2,1,0:T(8,128)(2,1)} %normals.1, f32[64,64]{1,0:T(8,128)} %chol.1, f32[1,64]{1,0:T(1,128)} %bitcast.7, f32[1,64]{1,0:T(1,128)} %bitcast.8, f32[64,128]{1,0:T(8,128)} %bmap.1, f32[1,128]{1,0:T(1,128)} %bitcast.9, bf16[128,1024]{1,0:T(8,128)(2,1)} %coef.1, s32[1,1024]{1,0:T(1,128)} %bitcast.5, ...), custom_call_target="tpu_custom_call" | custom-call | tf_op jit(solution)/shard_map/pallas_call | solution.py:361
  23.4 0.6 %copy.11 = f32[2,128]{1,0:T(2,128)} copy(f32[2,128]{1,0:T(2,128)S(1)} %shard_map.91) | data formatting | bytes 2048
